TPU v7x, 32 devices: a whole 2x2x4 slice. The times are simulated.
32 devices in a mesh: group: 2 (over x), tile: 16 (over z, y, core).
Axes of the slice: x: 2, y: 2, z: 4, core: 2. Of those that a mesh axis runs over, the one named last changes fastest.
Arguments:
- object_field: float32 [4, 2, 2048, 2048], P('group', None, 'tile'), parts along dimension 0, may hold values from -6 to 6
- probe: float32 [2, 256, 256], replicated, may hold values from -6 to 6
- measured: bfloat16 [64, 256, 256], P(('group', 'tile')), parts along dimension 0, may hold values from 0.099609375 to 3
- frame_table: int32 [64, 3], P(('group', 'tile')), parts along dimension 0, may hold values from 0 to 1792, as said below
- frame_count: int32 [32], P(('group', 'tile')), parts along dimension 0, may hold values from 0 to 2, as said below
Outputs:
- updated_object: float32 [4, 2, 2048, 2048], P('group', None, 'tile'), parts along dimension 0
- phase_map: float32 [4, 2048, 2048], P('group', 'tile'), parts along dimension 0
There are 2 independent parts, one for each index of `group`. A program takes and returns all parts, laid end to end along the dimension named above; an argument that names none is the same for every part. Nothing has to cross between parts.
Inputs may be any that keep to these rules, and one draw needn't show every extreme that they name: `frame_table`: per slot: the row offset is below 128, and the frame's rows d * 128 + offset to that plus 256 - 1 and columns lie inside the projection; the angle is below 2. Only the first frame_count[d] slots of device d are live. `frame_count`: exactly 2 on some device in every draw; zero on every device d with d * 128 > 1792.
All inputs are finite; a program needn't handle non-finite values.
Results may differ from a plain program's by a relative error of at most 0.0009.
Values may be sent and summed in bfloat16 or wider, within the bound.
A program may use at most 192 MiB of HBM per device.

v0:
```python
import math

import jax
import jax.numpy as jnp
from jax import lax
from jax.sharding import PartitionSpec as P

magnitude_floor = 0.5
soften_term = 0.5
screen_term = 0.0001
epsilon_term = 1e-06
exact_mode = lax.Precision.HIGHEST


def passed_along(x, axis, by):
    size = lax.axis_size(axis)
    pairs = [(i, i + by) for i in range(size) if 0 <= i + by < size]
    return lax.ppermute(x, axis, pairs)


def padded_2(cells, sides, width):
    for axis, dim in sides:
        count = lax.axis_size(axis)
        ends = count - 1
        head = lax.slice_in_dim(cells, 0, width, axis=dim)
        tail = lax.slice_in_dim(cells, cells.shape[dim] - width, cells.shape[dim], axis=dim)
        cells = jnp.concatenate(
            [
                lax.ppermute(tail, axis, [(i, (i + 1) % count) for i in range(ends)]),
                cells,
                lax.ppermute(head, axis, [((i + 1) % count, i) for i in range(ends)]),
            ],
            axis=dim,
        )
    return cells


def fourier_tables(frame_side):
    indices = jnp.arange(frame_side, dtype=jnp.int32)
    products = indices[:, None] * indices[None, :] % frame_side
    phases = products.astype(jnp.float32) * (-2.0 * math.pi / frame_side)
    norm_scale = 1.0 / math.sqrt(frame_side)
    return (
        (jnp.cos(phases) * norm_scale).astype(jnp.bfloat16),
        (jnp.sin(phases) * norm_scale).astype(jnp.bfloat16),
    )


def complex_left(table_re, table_im, operand):
    side = table_re.shape[0]
    stacked = jnp.concatenate([table_re, table_im], 0)
    joined = jnp.concatenate([operand[0], operand[1]], 1)
    products = jnp.dot(stacked, joined, preferred_element_type=jnp.float32)
    return jnp.stack(
        [
            products[:side, :side] - products[side:, side:],
            products[:side, side:] + products[side:, :side],
        ]
    )


def complex_right(operand, table_re, table_im):
    side = table_re.shape[0]
    stacked = jnp.concatenate([operand[0], operand[1]], 0)
    joined = jnp.concatenate([table_re, table_im], 1)
    products = jnp.dot(stacked, joined, preferred_element_type=jnp.float32)
    return jnp.stack(
        [
            products[:side, :side] - products[side:, side:],
            products[:side, side:] + products[side:, :side],
        ]
    )


def correct_frame(exit_field, magnitude, fourier):
    cos_part, sin_part = fourier
    half_spectrum = complex_left(cos_part, sin_part, exit_field).astype(jnp.bfloat16)
    spectrum = complex_right(half_spectrum, cos_part, sin_part)
    amplitude = jnp.sqrt(spectrum[0] * spectrum[0] + spectrum[1] * spectrum[1])
    factor = magnitude.astype(jnp.float32) / jnp.maximum(amplitude, magnitude_floor) - 1.0
    change = (spectrum * factor[None]).astype(jnp.bfloat16)
    half_back = complex_left(cos_part, -sin_part, change).astype(jnp.bfloat16)
    return complex_right(half_back, cos_part, -sin_part)


def exit_wave(probe, patch):
    object_part = patch.astype(jnp.float32)
    real_part = probe[0] * object_part[0] - probe[1] * object_part[1]
    imag_part = probe[0] * object_part[1] + probe[1] * object_part[0]
    return jnp.stack([real_part, imag_part]).astype(jnp.bfloat16)


def object_step(probe, correction, probe_peak):
    real_part = (probe[0] * correction[0] + probe[1] * correction[1]) / probe_peak
    imag_part = (probe[0] * correction[1] - probe[1] * correction[0]) / probe_peak
    return jnp.stack([real_part, imag_part])


def phase_bond(first_cell, second_cell):
    cross_term = first_cell[:, 0] * second_cell[:, 1] - first_cell[:, 1] * second_cell[:, 0]
    power_sum = (
        first_cell[:, 0] ** 2
        + first_cell[:, 1] ** 2
        + second_cell[:, 0] ** 2
        + second_cell[:, 1] ** 2
        + soften_term
    )
    return 2.0 * cross_term / power_sum


def cosine_rows(first_freq, block_rows, grid_side):
    freqs = first_freq + jnp.arange(block_rows, dtype=jnp.int32)
    pixels = jnp.arange(grid_side, dtype=jnp.int32)
    phases = (2 * pixels[None, :] + 1) * freqs[:, None] % (4 * grid_side)
    norm_scale = jnp.where(freqs == 0, math.sqrt(1.0 / grid_side), math.sqrt(2.0 / grid_side))
    return norm_scale[:, None] * jnp.cos(phases.astype(jnp.float32) * (math.pi / grid_side / 2.0))


def eigen_values(freqs, grid_side):
    return 2.0 - 2.0 * jnp.cos(freqs.astype(jnp.float32) * (math.pi / grid_side))


def body(object_field, probe, measured, frame_table, frame_count):
    angles, _, strip_rows, grid_side = object_field.shape
    frame_side = probe.shape[1]
    reach_count = frame_side // strip_rows
    live_count = frame_count[0]
    fourier = fourier_tables(frame_side)
    probe_peak = jnp.max(probe[0] * probe[0] + probe[1] * probe[1]) + epsilon_term
    anchor = jnp.zeros((), jnp.int32)
    own_strip = object_field.astype(jnp.bfloat16)
    growth = []
    window = own_strip
    covered = 1
    while covered < reach_count + 1:
        adding = min(covered, reach_count + 1 - covered)
        arrived = passed_along(window[:, :, : adding * strip_rows], "tile", -covered)
        window = jnp.concatenate([window, arrived], 2)
        growth.append((covered, adding))
        covered = covered + adding

    def extract(record):
        row_offset, column, angle_id = record
        patch = lax.dynamic_slice(
            window, (angle_id, anchor, row_offset, column), (1, 2, frame_side, frame_side)
        )[0]
        return exit_wave(probe, patch)

    patches = lax.map(extract, (frame_table[:, 0], frame_table[:, 1], frame_table[:, 2]))
    corrections = jax.vmap(
        lambda exit_field, magnitude: correct_frame(exit_field, magnitude, fourier)
    )(patches, measured)

    def deposit(slot_index, deposits):
        record = frame_table[slot_index]
        correction = lax.dynamic_index_in_dim(corrections, slot_index, 0, keepdims=False)
        update = object_step(probe, correction, probe_peak)
        corner = (record[2], anchor, record[0], record[1])
        current = lax.dynamic_slice(deposits, corner, (1, 2, frame_side, frame_side))
        return lax.dynamic_update_slice(deposits, current + update[None], corner)

    deposits = lax.fori_loop(0, live_count, deposit, jnp.zeros(window.shape, jnp.float32))
    for covered, adding in reversed(growth):
        piece = deposits[:, :, covered * strip_rows : (covered + adding) * strip_rows]
        arrived = passed_along(piece.astype(jnp.bfloat16), "tile", covered).astype(piece.dtype)
        deposits = jnp.concatenate(
            [
                deposits[:, :, : adding * strip_rows] + arrived,
                deposits[:, :, adding * strip_rows : covered * strip_rows],
            ],
            2,
        )
    updated_object = object_field + deposits
    extended = padded_2(updated_object, (("tile", 2),), 1)
    padded = jnp.pad(extended, ((0, 0), (0, 0), (0, 0), (1, 1)))
    row_grad = phase_bond(padded[:, :, :-1, 1:-1], padded[:, :, 1:, 1:-1])
    col_grad = phase_bond(padded[:, :, 1:-1, :-1], padded[:, :, 1:-1, 1:])
    source = -(row_grad[:, 1:] - row_grad[:, :-1] + col_grad[:, :, 1:] - col_grad[:, :, :-1])
    block_rows = min(512, grid_side)
    column_coeffs = jnp.concatenate(
        [
            jnp.einsum(
                "arn,kn->ark",
                source,
                cosine_rows(first_freq, block_rows, grid_side),
                precision=exact_mode,
            )
            for first_freq in range(0, grid_side, block_rows)
        ],
        2,
    )
    pencil = lax.all_to_all(column_coeffs, "tile", split_axis=2, concat_axis=1, tiled=True)
    width_here = pencil.shape[2]
    col_ids = lax.axis_index("tile") * width_here + jnp.arange(width_here, dtype=jnp.int32)
    col_eigen = eigen_values(col_ids, grid_side)
    solved = jnp.zeros(pencil.shape, jnp.float32)
    for solve_first_freq in range(0, grid_side, block_rows):
        solve_cos_block = cosine_rows(solve_first_freq, block_rows, grid_side)
        partial_value = jnp.einsum("ki,aij->akj", solve_cos_block, pencil, precision=exact_mode)
        row_eigen = eigen_values(
            solve_first_freq + jnp.arange(block_rows, dtype=jnp.int32), grid_side
        )
        partial_value = partial_value / (
            screen_term + row_eigen[None, :, None] + col_eigen[None, None, :]
        )
        solved = solved + jnp.einsum(
            "ki,akj->aij", solve_cos_block, partial_value, precision=exact_mode
        )
    row_solved = lax.all_to_all(solved, "tile", split_axis=1, concat_axis=2, tiled=True)
    phase_map = jnp.zeros(source.shape, jnp.float32)
    for first_freq in range(0, grid_side, block_rows):
        cos_block = cosine_rows(first_freq, block_rows, grid_side)
        phase_map = phase_map + jnp.einsum(
            "ark,kn->arn",
            row_solved[:, :, first_freq : first_freq + block_rows],
            cos_block,
            precision=exact_mode,
        )
    return (updated_object, phase_map)


def solution(mesh):
    return jax.shard_map(
        body,
        mesh=mesh,
        in_specs=(
            P("group", None, "tile", None),
            P(),
            P(("group", "tile"), None, None),
            P(("group", "tile"), None),
            P(("group", "tile")),
        ),
        out_specs=(P("group", None, "tile", None), P("group", "tile", None)),
        check_vma=False,
    )
```

profile of v0, /device:TPU:0, one launch (start us, length us, event | category | flops | bytes accessed | tf_op | source)
XLA Modules:
  0.0 670.3 jit_solution(14193901196056568718)
XLA Ops:
  9.8 67.4 %collective-permute-done.1 = bf16[2,2,128,2048]{3,2,1,0:T(8,128)(2,1)} collective-permute-done((bf16[2,2,128,2048]{3,2,1,0:T(8,128)(2,1)S(1)}, bf16[2,2,128,2048]{3,2,1,0:T(8,128)(2,1)}, u32[]{:S(2)}, u32[]{:S(2)}) %collective-permute-start.1) | collective-permute-done | bytes 2097184 | tf_op jit(solution)/shard_map/ppermute | solution.py:18
  82.6 17.7 %while.20 = (s32[]{:T(128)}, bf16[2,2,256,256]{3,2,0,1:T(8,128)(2,1)}, f32[2,256,256]{2,1,0:T(8,128)S(1)}, s32[2]{0:T(128)S(1)}, s32[2]{0:T(128)S(1)}, /*index=5...) while((s32[]{:T(128)}, ...), condition=%wide.region_1.2_spmd, body=%wide.region_0.1_spmd.sunk | while | flops 1179659 | bytes 2622219 | solution.py:149
  110.4 15.6 %while.21 = (s32[]{:T(128)}, f32[2,2,384,2048]{3,2,1,0:T(8,128)}, s32[]{:T(128)}, s32[2,3]{1,0:T(2,128)S(1)}, f32[2,256,256]{2,1,0:T(8,128)S(1)}, /*index=5*/f32...) while((s32[]{:T(128)}, f32[2,2,384,2048]{3,2,1,0:T(8,128)}, ...), condition=%wide.region_4.5_spmd, body=%wide.region_3.4_spmd.sunk | while | flops 786446 | bytes 5243209 | solution.py:162
  118.8 6.6 dynamic_update_slice.11
  137.7 44.4 %collective-permute-done.2 = bf16[2,2,128,2048]{3,2,1,0:T(8,128)(2,1)S(1)} collective-permute-done((bf16[2,2,128,2048]{3,2,1,0:T(8,128)(2,1)S(1)}, bf16[2,2,128,2048]{3,2,1,0:T(8,128)(2,1)S(1)}, u32[]{:S(2)}, u32[]{:S(2)}) %collective-permute-start.2) | collective-permute-done | bytes 2097184 | tf_op jit(solution)/shard_map/ppermute | solution.py:18
  208.4 19.2 %fusion.38 = f32[2,128,512]{2,1,0:T(8,128)S(1)} fusion(f32[2,128,2048]{2,1,0:T(8,128)S(1)} %fusion.86, s32[2048]{0:T(1024)S(1)} %multiply_add_fusion, f32[512]{0:T(512)S(1)} %fusion.272), kind=kOutput, calls=%fused_computation.74 | convolution fusion | flops 3236954112 | bytes 2631680 | tf_op jit(solution)/shard_map/arn,kn->ark/dot_general | solution.py:182
  227.6 19.6 %fusion.54 = f32[2,128,512]{2,1,0:T(8,128)S(1)} fusion(f32[2,128,2048]{2,1,0:T(8,128)S(1)} %fusion.86, s32[512]{0:T(512)S(1)} %iota_add_fusion.1, f32[512]{0:T(512)S(1)} %compare_select_fusion.1, s32[2048]{0:T(1024)S(1)} %multiply_add_fusion), kind=kOutput, calls=%fused_computation.82 | convolution fusion | flops 3236954112 | bytes 2633728 | tf_op jit(solution)/shard_map/arn,kn->ark/dot_general | solution.py:182
  247.2 19.2 %fusion.62 = f32[2,128,512]{2,1,0:T(8,128)S(1)} fusion(f32[2,128,2048]{2,1,0:T(8,128)S(1)} %fusion.86, s32[512]{0:T(512)S(1)} %iota_add_fusion.2, f32[512]{0:T(512)S(1)} %compare_select_fusion.2, s32[2048]{0:T(1024)S(1)} %multiply_add_fusion), kind=kOutput, calls=%fused_computation.86 | convolution fusion | flops 3236954112 | bytes 2633728 | tf_op jit(solution)/shard_map/arn,kn->ark/dot_general | solution.py:182
  266.4 19.6 %fusion.46 = f32[2,128,512]{2,1,0:T(8,128)S(1)} fusion(f32[2,128,2048]{2,1,0:T(8,128)S(1)} %fusion.86, s32[512]{0:T(512)S(1)} %iota_add_fusion, f32[512]{0:T(512)S(1)} %compare_select_fusion, s32[2048]{0:T(1024)S(1)} %multiply_add_fusion), kind=kOutput, calls=%fused_computation.78 | convolution fusion | flops 3236954112 | bytes 2633728 | tf_op jit(solution)/shard_map/arn,kn->ark/dot_general | solution.py:182
  288.5 22.8 %all-to-all-start = ((f32[2,128,2048]{1,0,2:T(2,128)}), f32[2,128,2048]{1,0,2:T(2,128)S(1)}, u32[]{:S(2)}, u32[]{:S(2)}) async-start(f32[2,128,2048]{1,0,2:T(2,128)} %copy.65), calls=%async_computation | async-start | bytes 4194304 | tf_op jit(solution)/shard_map/all_to_all | solution.py:192
  311.6 40.7 %all-to-all-done = f32[2,128,2048]{1,0,2:T(2,128)S(1)} async-done(((f32[2,128,2048]{1,0,2:T(2,128)}), f32[2,128,2048]{1,0,2:T(2,128)S(1)}, u32[]{:S(2)}, u32[]{:S(2)}) %all-to-all-start) | async-done | bytes 2097184 | tf_op jit(solution)/shard_map/all_to_all | solution.py:192
  355.6 22.5 %fusion.211 = f32[2,512,128]{1,2,0:T(8,128)S(1)} fusion(f32[2,2048,128]{2,1,0:T(8,128)S(1)} %bitcast.238, s32[512]{0:T(512)S(1)} %iota_add_fusion.1, f32[512]{0:T(512)S(1)} %compare_select_fusion.1, s32[2048]{0:T(1024)S(1)} %multiply_add_fusion, f32[512,128]{0,1:T(8,128)S(1)} %get-tuple-element.165), kind=kOutput, calls=%fused_computation.220 | convolution fusion | flops 3237085184 | bytes 2895872 | tf_op jit(solution)/shard_map/ki,aij->akj/dot_general | solution.py:199
  378.1 19.3 %fusion.50 = f32[2,128,2048]{2,1,0:T(8,128)S(1)} fusion(f32[2,512,128]{1,2,0:T(8,128)S(1)} %fusion.211, s32[512]{0:T(512)S(1)} %iota_add_fusion.1, f32[512]{0:T(512)S(1)} %compare_select_fusion.1, s32[2048]{0:T(1024)S(1)} %multiply_add_fusion), kind=kOutput, calls=%fused_computation.80 | convolution fusion | flops 3236954112 | bytes 2633728 | tf_op jit(solution)/shard_map/ki,akj->aij/dot_general | solution.py:206
  397.4 23.2 %fusion.217 = f32[2,512,128]{1,2,0:T(8,128)S(1)} fusion(f32[2,2048,128]{2,1,0:T(8,128)S(1)} %bitcast.239, s32[2048]{0:T(1024)S(1)} %multiply_add_fusion, f32[512]{0:T(512)S(1)} %fusion.272, f32[512,128]{0,1:T(8,128)S(1)} %get-tuple-element.167), kind=kOutput, calls=%fused_computation.222 | convolution fusion | flops 3237085184 | bytes 2893824 | tf_op jit(solution)/shard_map/ki,aij->akj/dot_general | solution.py:199
  420.6 19.3 %fusion.34 = f32[2,128,2048]{2,1,0:T(8,128)S(1)} fusion(f32[2,512,128]{1,2,0:T(8,128)S(1)} %fusion.217, s32[2048]{0:T(1024)S(1)} %multiply_add_fusion, f32[512]{0:T(512)S(1)} %fusion.272), kind=kOutput, calls=%fused_computation.72 | convolution fusion | flops 3236954112 | bytes 2631680 | tf_op jit(solution)/shard_map/ki,akj->aij/dot_general | solution.py:206
  439.9 23.1 %fusion.208 = f32[2,512,128]{1,2,0:T(8,128)S(1)} fusion(f32[2,2048,128]{2,1,0:T(8,128)S(1)} %bitcast.240, s32[512]{0:T(512)S(1)} %iota_add_fusion, f32[512]{0:T(512)S(1)} %compare_select_fusion, s32[2048]{0:T(1024)S(1)} %multiply_add_fusion, f32[512,128]{0,1:T(8,128)S(1)} %get-tuple-element.166), kind=kOutput, calls=%fused_computation.219 | convolution fusion | flops 3237085184 | bytes 2895872 | tf_op jit(solution)/shard_map/ki,aij->akj/dot_general | solution.py:199
  463.0 19.3 %fusion.42 = f32[2,128,2048]{2,1,0:T(8,128)S(1)} fusion(f32[2,512,128]{1,2,0:T(8,128)S(1)} %fusion.208, s32[512]{0:T(512)S(1)} %iota_add_fusion, f32[512]{0:T(512)S(1)} %compare_select_fusion, s32[2048]{0:T(1024)S(1)} %multiply_add_fusion), kind=kOutput, calls=%fused_computation.76 | convolution fusion | flops 3236954112 | bytes 2633728 | tf_op jit(solution)/shard_map/ki,akj->aij/dot_general | solution.py:206
  482.3 23.2 %fusion.214 = f32[2,512,128]{1,2,0:T(8,128)S(1)} fusion(f32[2,2048,128]{2,1,0:T(8,128)S(1)} %bitcast.241, s32[512]{0:T(512)S(1)} %iota_add_fusion.2, f32[512]{0:T(512)S(1)} %compare_select_fusion.2, s32[2048]{0:T(1024)S(1)} %multiply_add_fusion, f32[512,128]{0,1:T(8,128)S(1)} %get-tuple-element.164), kind=kOutput, calls=%fused_computation.221 | convolution fusion | flops 3237085184 | bytes 2895872 | tf_op jit(solution)/shard_map/ki,aij->akj/dot_general | solution.py:199
  505.5 20.8 %fusion.73 = f32[2,2048,128]{1,2,0:T(8,128)} fusion(f32[2,128,2048]{2,1,0:T(8,128)S(1)} %fusion.42, f32[2,128,2048]{2,1,0:T(8,128)S(1)} %fusion.50, f32[2,128,2048]{2,1,0:T(8,128)S(1)} %fusion.34, f32[2,512,128]{1,2,0:T(8,128)S(1)} %fusion.214, s32[512]{0:T(512)S(1)} %iota_add_fusion.2, f32[512]{0:T(512)S(1)} %compare_select_fusion.2, ...), kind=kOutput, calls=%fused_computation.90 | convolution fusion | flops 3238526976 | bytes 8925184 | tf_op jit(solution)/shard_map/ki,akj->aij/dot_general | solution.py:206
  529.2 58.2 %all_to_all.36 = f32[2,2048,128]{2,0,1:T(2,128)S(1)} all-to-all(f32[2,2048,128]{2,0,1:T(2,128)S(1)} %copy.72), channel_id=1, replica_groups=mesh['group'=2,'tile'=16] {'tile'}, dimensions={1} | all-to-all | bytes 4194304 | tf_op jit(solution)/shard_map/all_to_all | solution.py:209
  590.2 20.3 %fusion.48 = f32[2,128,2048]{2,1,0:T(8,128)S(1)} fusion(s32[512]{0:T(512)S(1)} %iota_add_fusion.1, f32[512]{0:T(512)S(1)} %compare_select_fusion.1, s32[2048]{0:T(1024)S(1)} %multiply_add_fusion, f32[2,128,2048]{2,1,0:T(8,128)} %all_to_all.33), kind=kOutput, calls=%fused_computation.79 | convolution fusion | flops 3236954112 | bytes 2633728 | tf_op jit(solution)/shard_map/ark,kn->arn/dot_general | solution.py:213
  610.5 19.5 %fusion.32 = f32[2,128,2048]{2,1,0:T(8,128)S(1)} fusion(s32[2048]{0:T(1024)S(1)} %multiply_add_fusion, f32[512]{0:T(512)S(1)} %fusion.272, f32[2,128,2048]{2,1,0:T(8,128)S(1)} %copy-done.3), kind=kOutput, calls=%fused_computation.71 | convolution fusion | flops 3236954112 | bytes 2631680 | tf_op jit(solution)/shard_map/ark,kn->arn/dot_general | solution.py:213
  630.0 19.1 %fusion.40 = f32[2,128,2048]{2,1,0:T(8,128)S(1)} fusion(s32[512]{0:T(512)S(1)} %iota_add_fusion, f32[512]{0:T(512)S(1)} %compare_select_fusion, s32[2048]{0:T(1024)S(1)} %multiply_add_fusion, f32[2,128,2048]{2,1,0:T(8,128)S(1)} %copy-done.3), kind=kOutput, calls=%fused_computation.75 | convolution fusion | flops 3236954112 | bytes 2633728 | tf_op jit(solution)/shard_map/ark,kn->arn/dot_general | solution.py:213
  649.1 21.0 %fusion.82 = f32[2,128,2048]{2,1,0:T(8,128)} fusion(f32[2,128,2048]{2,1,0:T(8,128)S(1)} %fusion.40, f32[2,128,2048]{2,1,0:T(8,128)S(1)} %fusion.48, f32[2,128,2048]{2,1,0:T(8,128)S(1)} %fusion.32, s32[512]{0:T(512)S(1)} %iota_add_fusion.2, f32[512]{0:T(512)S(1)} %compare_select_fusion.2, s32[2048]{0:T(1024)S(1)} %multiply_add_fusion, ...), kind=kOutput, calls=%fused_computation.93 | convolution fusion | flops 3238526976 | bytes 8925184 | tf_op jit(solution)/shard_map/ark,kn->arn/dot_general | solution.py:213
  (89 shorter events, 83.1 us)
Async XLA Ops:
  0.6 5.2 copy-start.4
  0.6 5.4 copy-start
  0.7 6.8 %copy-start.5 = (s32[2,3]{1,0:T(2,128)S(1)}, s32[2,3]{1,0:T(2,128)}, u32[]{:S(2)}) copy-start(s32[2,3]{1,0:T(2,128)} %param.12) | copy-start | bytes 76
  3.2 6.5 collective-permute-start
  4.5 72.7 %collective-permute-start.1 = (bf16[2,2,128,2048]{3,2,1,0:T(8,128)(2,1)S(1)}, bf16[2,2,128,2048]{3,2,1,0:T(8,128)(2,1)}, u32[]{:S(2)}, u32[]{:S(2)}) collective-permute-start(bf16[2,2,128,2048]{3,2,1,0:T(8,128)(2,1)S(1)} %convert_element_type.153), channel_id=1, source_target_pairs={{2,0},{3,1},{4,2},{5,3},{6,4},{7,5},{8,6},{9,7},{10,8},{11,9},{12,... | collective-permute-start | bytes 6291464 | tf_op jit(solution)/shard_map/ppermute | solution.py:18
  131.6 50.5 %copy-start.2 = (f32[2,2,128,2048]{3,2,1,0:T(8,128)S(1)}, f32[2,2,128,2048]{3,2,1,0:T(8,128)}, u32[]{:S(2)}) copy-start(f32[2,2,128,2048]{3,2,1,0:T(8,128)} %param.9) | copy-start | bytes 12582916
  131.9 50.2 %collective-permute-start.2 = (bf16[2,2,128,2048]{3,2,1,0:T(8,128)(2,1)S(1)}, bf16[2,2,128,2048]{3,2,1,0:T(8,128)(2,1)S(1)}, u32[]{:S(2)}, u32[]{:S(2)}) collective-permute-start(bf16[2,2,128,2048]{3,2,1,0:T(8,128)(2,1)S(1)} %get-tuple-element.145), channel_id=1, source_target_pairs={{0,2},{1,3},{2,4},{3,5},{4,6},{5,7},{6,8},{7,9},{8,10},{9,11},{10,... | collective-permute-start | bytes 6291464 | tf_op jit(solution)/shard_map/ppermute | solution.py:18
  136.2 45.9 %collective-permute-start.3 = (bf16[2,2,128,2048]{3,2,1,0:T(8,128)(2,1)S(1)}, bf16[2,2,128,2048]{3,2,1,0:T(8,128)(2,1)S(1)}, u32[]{:S(2)}, u32[]{:S(2)}) collective-permute-start(bf16[2,2,128,2048]{3,2,1,0:T(8,128)(2,1)S(1)} %get-tuple-element.146), channel_id=1, source_target_pairs={{0,1},{1,2},{2,3},{3,4},{4,5},{5,6},{6,7},{7,8},{8,9},{9,10},{10,1... | collective-permute-start | bytes 6291464 | tf_op jit(solution)/shard_map/ppermute | solution.py:18
  185.6 11.9 %copy-start.1 = (f32[2,2,128,2048]{3,2,1,0:T(8,128)}, f32[2,2,128,2048]{3,2,1,0:T(8,128)S(1)}, u32[]{:S(2)}) copy-start(f32[2,2,128,2048]{3,2,1,0:T(8,128)S(1)} %add_add_fusion) | copy-start | bytes 12582916
  191.3 5.9 collective-permute-start.5
  192.6 5.0 collective-permute-start.4
  288.5 63.7 %all-to-all-start = ((f32[2,128,2048]{1,0,2:T(2,128)}), f32[2,128,2048]{1,0,2:T(2,128)S(1)}, u32[]{:S(2)}, u32[]{:S(2)}) async-start(f32[2,128,2048]{1,0,2:T(2,128)} %copy.65), calls=%async_computation | async-start | bytes 4194304 | tf_op jit(solution)/shard_map/all_to_all | solution.py:192
  590.2 20.3 %copy-start.3 = (f32[2,128,2048]{2,1,0:T(8,128)S(1)}, f32[2,128,2048]{2,1,0:T(8,128)}, u32[]{:S(2)}) copy-start(f32[2,128,2048]{2,1,0:T(8,128)} %all_to_all.33) | copy-start | bytes 6291460
where the time goes:
time: 681 us; the launch traced here: 670 us
  matrix products  330 us (48%)
  waiting for transfers between devices  153 us (22%)
  blocking collectives  58.2 us (9%)
  local copies, waits for them, and re-layouts  37.4 us (5%)
  starting transfers between devices  36.9 us (5%)
  other arithmetic  35.8 us (5%)
  loops' own time  17.2 us (3%)
    ppermute x4, waiting for transfers between devices, passed_along(): return lax.ppermute(x, axis, pairs)  112 us
    dot_general x4, matrix products, body(): jnp.einsum('ki,aij->akj', solve_cos_block, pencil, precision=exact_mode)  92 us
    dot_general x4, matrix products, body(): jnp.einsum('ark,kn->arn', row_solved[:, :, first_freq:first_freq + block_...  79.8 us
    dot_general x4, matrix products, body(): jnp.einsum('ki,akj->aij', solve_cos_block, partial_value, precision=exact...  78.7 us
    dot_general x4, matrix products, body(): jnp.einsum('arn,kn->ark', source, cosine_rows(first_freq, block_rows, gri...  77.6 us
    all_to_all x1, blocking collectives, body(): lax.all_to_all(solved, 'tile', split_axis=1, concat_axis=2, tiled=True)  58.2 us
    all_to_all x1, waiting for transfers between devices, body(): lax.all_to_all(column_coeffs, 'tile', split_axis=2, concat_axis=1, tiled=...  40.7 us
    all_to_all x1, starting transfers between devices, body(): lax.all_to_all(column_coeffs, 'tile', split_axis=2, concat_axis=1, tiled=...  22.8 us
  transfers between devices with their start and end apart: 7, of which 4 were waited for; matrix products, arithmetic and copies ran while one was open for 1% of the time, Pallas kernels for 0%

commit v1 on v0

v1 whole, which is shorter than its diff:
```python
import functools
import math

import numpy as np
import jax
import jax.numpy as jnp
from jax import lax
from jax.experimental import pallas as pl
from jax.experimental.pallas import tpu as pltpu
from jax.sharding import PartitionSpec as P

magnitude_floor = 0.5
soften_term = 0.5
screen_term = 0.0001
epsilon_term = 1e-06
f32 = jnp.float32
bf16 = jnp.bfloat16
LANES = 128
GROUP = 8
TILE = 256
VMEM_BYTES = 60 * 1024 * 1024
vmem = pl.BlockSpec(memory_space=pltpu.VMEM)
smem = pl.BlockSpec(memory_space=pltpu.SMEM)
hbm = pl.BlockSpec(memory_space=pl.ANY)


def passed_along(x, axis, by):
    size = lax.axis_size(axis)
    pairs = [(i, i + by) for i in range(size) if 0 <= i + by < size]
    return lax.ppermute(x, axis, pairs)


def params(**more):
    return pltpu.CompilerParams(vmem_limit_bytes=VMEM_BYTES, **more)


def fourier_tables(side):
    indices = np.arange(side)
    products = indices[:, None] * indices[None, :] % side
    phases = products.astype(np.float64) * (-2.0 * math.pi / side)
    scale = 1.0 / math.sqrt(side)
    return (
        jnp.asarray(np.cos(phases) * scale, f32).astype(bf16),
        jnp.asarray(np.sin(phases) * scale, f32).astype(bf16),
    )


def cosine_factors(grid_side):
    half = grid_side // 2
    step = 32
    out = []
    for odd in (0, 1):
        freqs = 2 * np.arange(half) + odd
        scale = np.where(freqs == 0, math.sqrt(1.0 / grid_side), math.sqrt(2.0 / grid_side))
        coarse = (2 * step * np.arange(half // step)[:, None] * freqs[None, :]) % (4 * grid_side)
        fine = ((2 * np.arange(step)[:, None] + 1) * freqs[None, :]) % (4 * grid_side)
        unit = math.pi / (2 * grid_side)
        out.append(
            np.stack(
                [
                    np.cos(coarse * unit) * scale,
                    np.sin(coarse * unit) * scale,
                    np.cos(fine * unit),
                    np.sin(fine * unit),
                ]
            )
        )
    return jnp.asarray(np.stack(out), f32)


def decay_tables(grid_side, strip_rows):
    half = grid_side // 2
    freqs = np.concatenate([2 * np.arange(half), 2 * np.arange(half) + 1]).astype(np.float64)
    shift = screen_term + 2.0 - 2.0 * np.cos(freqs * math.pi / grid_side)
    rate = 2.0 * np.arcsinh(np.sqrt(shift) / 2.0)
    gain = 1.0 / (2.0 * np.sinh(rate))
    rows = np.arange(GROUP)[:, None]
    down = [np.where(rows >= s, np.exp(-s * rate), 0.0) for s in (1, 2, 4)]
    up = [np.where(rows < GROUP - s, np.exp(-s * rate), 0.0) for s in (1, 2, 4)]
    down.append(np.exp(-(rows + 1) * rate))
    up.append(np.exp(-(GROUP - rows) * rate))
    local = np.stack(down + up)
    strips = grid_side // strip_rows
    powers = np.exp(-strip_rows * np.arange(strips + 1)[:, None] * rate)
    extra = np.stack(
        [gain, 1.0 / (1.0 - np.exp(-2.0 * grid_side * rate)), np.exp(-GROUP * rate)]
        + [rate * 0.0] * 5
    )
    return jnp.asarray(local, f32), jnp.asarray(powers, f32), jnp.asarray(extra, f32)


def table_kernel(factors, even_hi, even_lo, odd_hi, odd_lo):
    step = factors.shape[2]
    blocks = even_hi.shape[0] // step
    for part, (high, low) in enumerate(((even_hi, even_lo), (odd_hi, odd_lo))):
        fine_cos = factors[part, 2]
        fine_sin = factors[part, 3]
        for block in range(blocks):
            value = (
                factors[part, 0, block : block + 1] * fine_cos
                - factors[part, 1, block : block + 1] * fine_sin
            )
            rounded = value.astype(bf16)
            high[block * step : (block + 1) * step] = rounded
            low[block * step : (block + 1) * step] = (value - rounded.astype(f32)).astype(bf16)


def window_start(column, width, span):
    return jnp.minimum(column // LANES, (width - span) // LANES) * LANES


def cut_kernel(tables, field, out, buffer, sems):
    count, cap = tables.shape[0], tables.shape[1]
    width = field.shape[3]
    side = out.shape[-1]
    span = side + LANES
    jobs = [(j, s) for j in range(count) for s in range(cap)]

    def fetch(index):
        j, s = jobs[index]
        start = pl.multiple_of(window_start(tables[j, s, 1], width, span), LANES)
        return pltpu.make_async_copy(
            field.at[tables[j, s, 2], :, :, pl.ds(start, span)], buffer.at[index], sems.at[index]
        )

    for index in range(len(jobs)):
        fetch(index).start()
    for index, (j, s) in enumerate(jobs):
        fetch(index).wait()
        column = tables[j, s, 1]
        shift = column - window_start(column, width, span)
        for part in range(2):
            turned = pltpu.roll(buffer[index, part], lax.rem(span - shift, span), 1)
            out[j, s, part] = turned[:, :side].astype(bf16)


def frame_kernel(table, counts, probe, measured, cos_ref, sin_ref, *refs):
    pieces = refs[: len(refs) - 3]
    own_out, away_out, window = refs[len(refs) - 3 :]
    cap, side = measured.shape[0], measured.shape[1]
    strip = pieces[0].shape[2]
    reach = len(pieces) - 1
    total = (reach + 1) * strip
    cos_part, sin_part = cos_ref[...], sin_ref[...]
    stacked = jnp.concatenate([cos_part, sin_part], 0)
    joined = jnp.concatenate([cos_part, sin_part], 1)
    probe_re, probe_im = probe[0], probe[1]
    peak = jnp.max(probe_re * probe_re + probe_im * probe_im) + epsilon_term

    def left(re, im, sign):
        products = jnp.dot(
            stacked, jnp.concatenate([re, im], 1), preferred_element_type=f32
        )
        cc, ci = products[:side, :side], products[:side, side:]
        sc, si = products[side:, :side], products[side:, side:]
        return (cc - si, ci + sc) if sign > 0 else (cc + si, ci - sc)

    def right(re, im, sign):
        products = jnp.dot(
            jnp.concatenate([re, im], 0), joined, preferred_element_type=f32
        )
        rc, rs = products[:side, :side], products[:side, side:]
        ic, js = products[side:, :side], products[side:, side:]
        return (rc - js, rs + ic) if sign > 0 else (rc + js, ic - rs)

    for s in range(cap):
        offset = table[s, 0]
        patch = []
        for part in range(2):
            for j in range(reach + 1):
                window[j * strip : (j + 1) * strip] = pieces[j][s, part].astype(f32)
            turned = pltpu.roll(window[...], lax.rem(total - offset, total), 0)
            patch.append(turned[:side])
        wave_re = (probe_re * patch[0] - probe_im * patch[1]).astype(bf16)
        wave_im = (probe_re * patch[1] + probe_im * patch[0]).astype(bf16)
        half_re, half_im = left(wave_re, wave_im, 1)
        spec_re, spec_im = right(half_re.astype(bf16), half_im.astype(bf16), 1)
        amplitude = jnp.sqrt(spec_re * spec_re + spec_im * spec_im)
        factor = measured[s].astype(f32) / jnp.maximum(amplitude, magnitude_floor) - 1.0
        back_re, back_im = left(
            (spec_re * factor).astype(bf16), (spec_im * factor).astype(bf16), -1
        )
        corr_re, corr_im = right(back_re.astype(bf16), back_im.astype(bf16), -1)
        live = s < counts[0]
        updates = (
            (probe_re * corr_re + probe_im * corr_im) / peak,
            (probe_re * corr_im - probe_im * corr_re) / peak,
        )
        for part in range(2):
            window[...] = jnp.zeros_like(window)
            window[:side] = jnp.where(live, updates[part], 0.0)
            turned = pltpu.roll(window[...], offset, 0)
            own_out[s, part] = turned[:strip]
            for j in range(1, reach + 1):
                away_out[j - 1, s, part] = turned[j * strip : (j + 1) * strip].astype(bf16)


def place_kernel(tables, field, own, *refs):
    away, out = refs[:-1], refs[-1]
    width = field.shape[3]
    cap, side = own.shape[0], own.shape[3]
    span = side + LANES
    out[...] = field[...]
    pad = jnp.zeros((own.shape[2], LANES), f32)
    for j, source in enumerate((own, *away)):
        for s in range(cap):
            column = tables[j, s, 1]
            start = pl.multiple_of(window_start(column, width, span), LANES)
            shift = column - start
            angle = tables[j, s, 2]
            for part in range(2):
                value = jnp.concatenate([source[s, part].astype(f32), pad], 1)
                turned = pltpu.roll(value, shift, 1)
                out[angle, part, :, pl.ds(start, span)] = (
                    out[angle, part, :, pl.ds(start, span)] + turned
                )


def mirror(value):
    side = value.shape[1]
    rows = lax.broadcasted_iota(jnp.int32, (side, side), 0)
    columns = lax.broadcasted_iota(jnp.int32, (side, side), 1)
    swap = jnp.where(rows + columns == side - 1, 1.0, 0.0).astype(bf16)
    total = None
    for _ in range(3):
        piece = value.astype(bf16)
        value = value - piece.astype(f32)
        term = jnp.dot(piece, swap, preferred_element_type=f32)
        total = term if total is None else total + term
    return total


def split_store(value, high, low, columns):
    rounded = value.astype(bf16)
    high[:, columns] = rounded
    low[:, columns] = (value - rounded.astype(f32)).astype(bf16)


def bond(a_re, a_im, b_re, b_im):
    cross = a_re * b_im - a_im * b_re
    power = a_re * a_re + a_im * a_im + b_re * b_re + b_im * b_im + soften_term
    return 2.0 * cross / power


def forward_kernel(
    field, above, below, even_hi, even_lo, odd_hi, odd_lo, local, extra,
    out, ends, source, xeh, xel, xoh, xol,
):
    angles, _, strip, width = field.shape
    half = width // 2
    block = GROUP * 2
    columns = lax.broadcasted_iota(jnp.int32, (block, width), 1)
    for angle in range(angles):
        for first in range(0, strip, block):
            here, up, down, left = [], [], [], []
            for part in range(2):
                body = field[angle, part, first : first + block]
                before = (
                    above[angle, part]
                    if first == 0
                    else field[angle, part, first - 1 : first]
                )
                after = (
                    below[angle, part]
                    if first + block == strip
                    else field[angle, part, first + block : first + block + 1]
                )
                here.append(body)
                up.append(jnp.concatenate([before, body[:-1]], 0))
                down.append(jnp.concatenate([body[1:], after], 0))
                left.append(jnp.where(columns == 0, 0.0, pltpu.roll(body, 1, 1)))
            row_up = bond(*up, *here)
            row_down = bond(*here, *down)
            col_left = bond(*left, *here)
            col_right = jnp.where(
                columns == width - 1, 0.0, pltpu.roll(col_left, width - 1, 1)
            )
            source[angle * strip + first : angle * strip + first + block] = -(
                row_down - row_up + col_right - col_left
            )
    for first in range(0, half, TILE):
        near = source[:, first : first + TILE]
        far = mirror(source[:, width - first - TILE : width - first])
        where = slice(first, first + TILE)
        split_store(near + far, xeh, xel, where)
        split_store(near - far, xoh, xol, where)
    for base, high, low, table_hi, table_lo in (
        (0, xeh, xel, even_hi, even_lo),
        (half, xoh, xol, odd_hi, odd_lo),
    ):
        for first in range(0, half, TILE):
            where = slice(first, first + TILE)
            source[:, base + first : base + first + TILE] = (
                jnp.dot(high[...], table_hi[:, where], preferred_element_type=f32)
                + jnp.dot(low[...], table_hi[:, where], preferred_element_type=f32)
                + jnp.dot(high[...], table_lo[:, where], preferred_element_type=f32)
            )
    groups = strip // GROUP
    for first in range(0, width, LANES):
        where = slice(first, first + LANES)
        gain = extra[0:1, where]
        for angle in range(angles):
            value = source[angle * strip : (angle + 1) * strip, where]
            value = value.reshape(groups, GROUP, LANES)
            fall, rise = value, value
            for index, by in enumerate((1, 2, 4)):
                fall = fall + local[index, :, where][None] * pltpu.roll(fall, by, 1)
                rise = rise + local[4 + index, :, where][None] * pltpu.roll(rise, GROUP - by, 1)
            falls, carry = [], None
            for group in range(groups):
                item = fall[group]
                if carry is not None:
                    item = item + local[3, :, where] * carry
                carry = item[GROUP - 1 :]
                falls.append(item)
            ends[0, angle : angle + 1, where] = carry
            rises, carry = [None] * groups, None
            for group in reversed(range(groups)):
                item = rise[group]
                if carry is not None:
                    item = item + local[7, :, where] * carry
                carry = item[:1]
                rises[group] = item
            ends[1, angle : angle + 1, where] = carry
            for group in range(groups):
                out[angle, group * GROUP : (group + 1) * GROUP, where] = gain * (
                    falls[group] + rises[group] - value[group]
                )


def inverse_kernel(
    place, value, ends, even_hi, even_lo, odd_hi, odd_lo, local, powers, extra,
    out, incoming, xh, xl,
):
    angles, strip, width = value.shape
    half = width // 2
    strips = ends.shape[0]
    me = place[0]
    wall = jnp.zeros((angles, width), f32)
    floor = jnp.zeros((angles, width), f32)
    enter = jnp.zeros((angles, width), f32)
    leave = jnp.zeros((angles, width), f32)
    for b in range(strips):
        right_end, left_end = ends[b, 0], ends[b, 1]
        wall = wall + powers[b : b + 1] * left_end
        floor = floor + powers[strips - 1 - b : strips - b] * right_end
        weight = powers[pl.ds(jnp.maximum(me - 1 - b, 0), 1)]
        enter = enter + jnp.where(b < me, weight, 0.0) * right_end
        weight = powers[pl.ds(jnp.maximum(b - me - 1, 0), 1)]
        leave = leave + jnp.where(b > me, weight, 0.0) * left_end
    whole = powers[strips : strips + 1]
    closing = extra[1:2]
    gain = extra[0:1]
    enter = enter + powers[pl.ds(me, 1)] * (wall + whole * floor) * closing
    leave = leave + powers[pl.ds(strips - 1 - me, 1)] * (floor + whole * wall) * closing
    incoming[0] = enter * gain
    incoming[1] = leave * gain
    groups = strip // GROUP
    for first in range(0, width, LANES):
        where = slice(first, first + LANES)
        for angle in range(angles):
            fall = incoming[0, angle : angle + 1, where]
            rise = incoming[1, angle : angle + 1, where]
            step = extra[2:3, where]
            falls, rises = [], []
            for group in range(groups):
                falls.append(fall)
                rises.append(rise)
                fall = fall * step
                rise = rise * step
            for pair in range(0, groups, 2):
                rows = []
                for group in (pair, pair + 1):
                    rows.append(
                        value[angle, group * GROUP : (group + 1) * GROUP, where]
                        + local[3, :, where] * falls[group]
                        + local[7, :, where] * rises[groups - 1 - group]
                    )
                item = jnp.concatenate(rows, 0)
                rounded = item.astype(bf16)
                start = angle * strip + pair * GROUP
                xh[start : start + 2 * GROUP, where] = rounded
                xl[start : start + 2 * GROUP, where] = (item - rounded.astype(f32)).astype(bf16)
    last = (((1,), (1,)), ((), ()))
    for first in range(0, half, TILE):
        where = slice(first, first + TILE)
        parts = []
        for base, table_hi, table_lo in ((0, even_hi, even_lo), (half, odd_hi, odd_lo)):
            high = xh[:, base : base + half]
            low = xl[:, base : base + half]
            parts.append(
                lax.dot_general(high, table_hi[where], last, preferred_element_type=f32)
                + lax.dot_general(low, table_hi[where], last, preferred_element_type=f32)
                + lax.dot_general(high, table_lo[where], last, preferred_element_type=f32)
            )
        near = parts[0] + parts[1]
        far = mirror(parts[0] - parts[1])
        for angle in range(angles):
            rows = slice(angle * strip, (angle + 1) * strip)
            out[angle, :, where] = near[rows]
            out[angle, :, width - first - TILE : width - first] = far[rows]


def body(object_field, probe, measured, frame_table, frame_count):
    angles, _, strip, width = object_field.shape
    side = probe.shape[1]
    cap = measured.shape[0]
    half = width // 2
    reach = side // strip
    rows = angles * strip
    shape = jax.ShapeDtypeStruct

    above_tables = [frame_table] + [
        passed_along(frame_table, "tile", j) for j in range(1, reach + 1)
    ]
    tables = jnp.stack(above_tables)
    cuts = pl.pallas_call(
        cut_kernel,
        out_shape=shape((reach + 1, cap, 2, strip, side), bf16),
        in_specs=[smem, hbm],
        out_specs=vmem,
        scratch_shapes=[
            pltpu.VMEM(((reach + 1) * cap, 2, strip, side + LANES), f32),
            pltpu.SemaphoreType.DMA(((reach + 1) * cap,)),
        ],
        compiler_params=params(),
        name="cut",
    )(tables, object_field)
    pieces = [cuts[0]] + [passed_along(cuts[j], "tile", -j) for j in range(1, reach + 1)]

    factors = cosine_factors(width)
    half_tables = pl.pallas_call(
        table_kernel,
        out_shape=[shape((half, half), bf16)] * 4,
        in_specs=[vmem],
        out_specs=[vmem] * 4,
        compiler_params=params(),
        cost_estimate=pl.CostEstimate(
            flops=half * half * 10, bytes_accessed=half * half * 8, transcendentals=0
        ),
        name="tables",
    )(factors)
    local, powers, extra = decay_tables(width, strip)
    cos_part, sin_part = fourier_tables(side)

    own, away = pl.pallas_call(
        frame_kernel,
        out_shape=[
            shape((cap, 2, strip, side), f32),
            shape((reach, cap, 2, strip, side), bf16),
        ],
        in_specs=[smem, smem] + [vmem] * (5 + reach),
        out_specs=[vmem, vmem],
        scratch_shapes=[pltpu.VMEM(((reach + 1) * strip, side), f32)],
        compiler_params=params(),
        name="frames",
    )(frame_table, frame_count, probe, measured, cos_part, sin_part, *pieces)
    arrived = [passed_along(away[j - 1], "tile", j) for j in range(1, reach + 1)]

    updated = pl.pallas_call(
        place_kernel,
        out_shape=shape(object_field.shape, f32),
        in_specs=[smem, vmem, vmem] + [vmem] * reach,
        out_specs=vmem,
        compiler_params=params(),
        name="place",
    )(tables, object_field, own, *arrived)
    above = passed_along(updated[:, :, strip - 1 :], "tile", 1)
    below = passed_along(updated[:, :, :1], "tile", -1)

    solved, ends = pl.pallas_call(
        forward_kernel,
        out_shape=[shape((angles, strip, width), f32), shape((2, angles, width), f32)],
        in_specs=[vmem] * 9,
        out_specs=[vmem, vmem],
        scratch_shapes=[pltpu.VMEM((rows, width), f32)] + [pltpu.VMEM((rows, half), bf16)] * 4,
        compiler_params=params(),
        name="forward",
    )(updated, above, below, *half_tables, local, extra)
    every_end = lax.all_gather(ends, "tile")
    place = lax.axis_index("tile").astype(jnp.int32).reshape(1)
    phase_map = pl.pallas_call(
        inverse_kernel,
        out_shape=shape((angles, strip, width), f32),
        in_specs=[smem] + [vmem] * 9,
        out_specs=vmem,
        scratch_shapes=[
            pltpu.VMEM((2, angles, width), f32),
            pltpu.VMEM((rows, width), bf16),
            pltpu.VMEM((rows, width), bf16),
        ],
        compiler_params=params(),
        name="inverse",
    )(place, solved, every_end, *half_tables, local, powers, extra)
    return (updated, phase_map)


def solution(mesh):
    return jax.shard_map(
        body,
        mesh=mesh,
        in_specs=(
            P("group", None, "tile", None),
            P(),
            P(("group", "tile"), None, None),
            P(("group", "tile"), None),
            P(("group", "tile")),
        ),
        out_specs=(P("group", None, "tile", None), P("group", "tile", None)),
        check_vma=False,
    )
```

time: 681 us -> 120 us (0.18); the launches traced: 670 us -> 120 us
  matrix products: 330 us -> 0 us
  waiting for transfers between devices: 153 us -> 10.4 us
  Pallas kernels: 0 us -> 47.5 us
  other arithmetic: 35.8 us -> 1.27 us
  blocking collectives: 58.2 us -> 26.6 us
  local copies, waits for them, and re-layouts: 37.4 us -> 6.07 us
  loops' own time: 17.2 us -> 0 us
  starting transfers between devices: 36.9 us -> 26.4 us
    dot_general x20 -> x0, matrix products: 330 us -> none  [the longest x4 92 us: body(): jnp.einsum('ki,aij->akj', solve_cos_block, pencil, precision=exact_mode)]
    ppermute x4 -> x8, waiting for transfers between devices: 112 us -> 10.4 us  [passed_along(): return lax.ppermute(x, axis, pairs)]
    all_to_all x1 -> x0, blocking collectives: 58.2 us -> none  [body(): lax.all_to_all(solved, 'tile', split_axis=1, concat_axis=2, tiled=True)]
    pallas_call x0 -> x6, Pallas kernels: none -> 47.5 us  [the longest x1 15.6 us: body(): pl.pallas_call(forward_kernel, out_shape=[shape((angles, strip, width), f...]
    all_to_all x1 -> x0, waiting for transfers between devices: 40.7 us -> none  [body(): lax.all_to_all(column_coeffs, 'tile', split_axis=2, concat_axis=1, tiled=...]
    all_gather x0 -> x1, blocking collectives: none -> 26.6 us  [body(): every_end = lax.all_gather(ends, 'tile')]
    all_to_all x1 -> x0, starting transfers between devices: 22.8 us -> none  [body(): lax.all_to_all(column_coeffs, 'tile', split_axis=2, concat_axis=1, tiled=...]
    ppermute x4 -> x8, starting transfers between devices: 8.31 us -> 26.4 us  [passed_along(): return lax.ppermute(x, axis, pairs)]
  transfers between devices with their start and end apart: 7 -> 8, of which waited for: 4 -> 4; matrix products, arithmetic and copies ran while one was open for 1% -> 0% of each run, Pallas kernels for 0% -> 5%
where the time goes in v1:
time: 120 us
  Pallas kernels  47.5 us (40%)
  blocking collectives  26.6 us (22%)
  starting transfers between devices  26.4 us (22%)
  waiting for transfers between devices  10.4 us (9%)
  local copies, waits for them, and re-layouts  6.07 us (5%)
  between operations  1.39 us (1%)
  other arithmetic  1.27 us (1%)
    all_gather x1, blocking collectives, body(): every_end = lax.all_gather(ends, 'tile')  26.6 us
    ppermute x8, starting transfers between devices, passed_along(): return lax.ppermute(x, axis, pairs)  26.4 us
    pallas_call x1, Pallas kernels, body(): pl.pallas_call(forward_kernel, out_shape=[shape((angles, strip, width), f...  15.6 us
    pallas_call x1, Pallas kernels, body(): pl.pallas_call(inverse_kernel, out_shape=shape((angles, strip, width), f3...  11.5 us
    ppermute x8, waiting for transfers between devices, passed_along(): return lax.ppermute(x, axis, pairs)  10.4 us
    pallas_call x1, Pallas kernels, body(): pl.pallas_call(frame_kernel, out_shape=[shape((cap, 2, strip, side), f32)...  6.04 us
    pallas_call x1, Pallas kernels, body(): pl.pallas_call(table_kernel, out_shape=[shape((half, half), bf16)] * 4, i...  5.41 us
    pallas_call x1, Pallas kernels, body(): pl.pallas_call(place_kernel, out_shape=shape(object_field.shape, f32), in...  5.22 us
  transfers between devices with their start and end apart: 8, of which 4 were waited for; matrix products, arithmetic and copies ran while one was open for 0% of the time, Pallas kernels for 5%

profile of v1, /device:TPU:0, one launch (start us, length us, event | category | flops | bytes accessed | tf_op | source)
XLA Modules:
  0.0 119.6 jit_solution(2783605381073375660)
XLA Ops:
  0.6 2.4 %collective-permute-start = (s32[2,3]{1,0:T(2,128)}, s32[2,3]{1,0:T(2,128)S(1)}, u32[]{:S(2)}, u32[]{:S(2)}) collective-permute-start(s32[2,3]{1,0:T(2,128)} %table.1), channel_id=1, source_target_pairs={{0,1},{1,2},{2,3},{3,4},{4,5},{5,6},{6,7},{7,8},{8,9},{9,10},{10,1... | collective-permute-start | bytes 80 | tf_op jit(solution)/shard_map/ppermute | solution.py:30
  3.0 4.4 %collective-permute-start.1 = (s32[2,3]{1,0:T(2,128)}, s32[2,3]{1,0:T(2,128)S(1)}, u32[]{:S(2)}, u32[]{:S(2)}) collective-permute-start(s32[2,3]{1,0:T(2,128)} %table.1), channel_id=1, source_target_pairs={{0,2},{1,3},{2,4},{3,5},{4,6},{5,7},{6,8},{7,9},{8,10},{9,11},{10,... | collective-permute-start | bytes 80 | tf_op jit(solution)/shard_map/ppermute | solution.py:30
  7.5 1.5 %collective-permute-done.1 = s32[2,3]{1,0:T(2,128)S(1)} collective-permute-done((s32[2,3]{1,0:T(2,128)}, s32[2,3]{1,0:T(2,128)S(1)}, u32[]{:S(2)}, u32[]{:S(2)}) %collective-permute-start.1) | collective-permute-done | bytes 56 | tf_op jit(solution)/shard_map/ppermute | solution.py:30
  9.0 1.3 %pad_add_fusion.tables = s32[3,2,3]{2,1,0:T(2,128)} fusion(s32[1,2,3]{2,1,0:T(2,128)S(1)} %bitcast.18, s32[1,2,3]{2,1,0:T(2,128)S(1)} %bitcast.17, s32[1,2,3]{2,1,0:T(2,128)} %bitcast.16), kind=kLoop, calls=%fused_computation.5 | loop fusion | flops 36 | bytes 144 | tf_op jit(solution)/shard_map/stack | solution.py:416
  10.2 3.7 %cut.1 = bf16[3,2,2,128,256]{4,3,2,1,0:T(8,128)(2,1)} custom-call(s32[3,2,3]{2,1,0:T(2,128)} %pad_add_fusion.tables, f32[2,2,128,2048]{3,2,1,0:T(8,128)} %field.3), custom_call_target="tpu_custom_call" | custom-call | tf_op jit(solution)/shard_map/cut/pallas_call | solution.py:417
  13.9 1.9 %slice_bitcast_fusion = (bf16[2,2,128,256]{3,2,1,0:T(8,128)(2,1)S(1)}, bf16[2,2,128,256]{3,2,1,0:T(8,128)(2,1)S(1)}, bf16[2,2,128,256]{3,2,1,0:T(8,128)(2,1)}) fusion(bf16[3,2,2,128,256]{4,3,2,1,0:T(8,128)(2,1)} %cut.1), kind=kLoop, calls=%fused_computation | loop fusion | bytes 1572864 | tf_op jit(solution)/shard_map/squeeze | solution.py:429
  15.8 1.3 %collective-permute-start.3 = (bf16[2,2,128,256]{3,2,1,0:T(8,128)(2,1)S(1)}, bf16[2,2,128,256]{3,2,1,0:T(8,128)(2,1)S(1)}, u32[]{:S(2)}, u32[]{:S(2)}) collective-permute-start(bf16[2,2,128,256]{3,2,1,0:T(8,128)(2,1)S(1)} %get-tuple-element.20), channel_id=1, source_target_pairs={{2,0},{3,1},{4,2},{5,3},{6,4},{7,5},{8,6},{9,7},{10,8},{11,9},{12,... | collective-permute-start | bytes 786440 | tf_op jit(solution)/shard_map/ppermute | solution.py:30
  17.1 1.3 %collective-permute-start.2 = (bf16[2,2,128,256]{3,2,1,0:T(8,128)(2,1)S(1)}, bf16[2,2,128,256]{3,2,1,0:T(8,128)(2,1)S(1)}, u32[]{:S(2)}, u32[]{:S(2)}) collective-permute-start(bf16[2,2,128,256]{3,2,1,0:T(8,128)(2,1)S(1)} %get-tuple-element.21), channel_id=1, source_target_pairs={{1,0},{2,1},{3,2},{4,3},{5,4},{6,5},{7,6},{8,7},{9,8},{10,9},{11,1... | collective-permute-start | bytes 786440 | tf_op jit(solution)/shard_map/ppermute | solution.py:30
  19.0 7.8 %collective-permute-done.3.refs_2_ = bf16[2,2,128,256]{3,2,1,0:T(8,128)(2,1)S(1)} collective-permute-done((bf16[2,2,128,256]{3,2,1,0:T(8,128)(2,1)S(1)}, bf16[2,2,128,256]{3,2,1,0:T(8,128)(2,1)S(1)}, u32[]{:S(2)}, u32[]{:S(2)}) %collective-permute-start.3) | collective-permute-done | bytes 262176 | tf_op jit(solution)/shard_map/ppermute | solution.py:30
  26.8 0.7 copy-done.2
  27.6 6.0 %frames.1 = (f32[2,2,128,256]{3,2,1,0:T(8,128)}, bf16[2,2,2,128,256]{4,3,2,1,0:T(8,128)(2,1)}) custom-call(s32[2,3]{1,0:T(2,128)} %table.1, s32[1]{0:T(128)S(6)} %copy.13.counts, f32[2,256,256]{2,1,0:T(8,128)} %probe.1, bf16[2,256,256]{2,1,0:T(8,128)(2,1)} %measured.1, bf16[256,256]{1,0:T(8,128)(2,1)} %constant.25.cos_ref, ...), custom_call_target="tpu_custom_call" | custom-call | tf_op jit(solution)/shard_map/frames/pallas_call | solution.py:446
  33.6 1.1 slice_bitcast_fusion.3
  34.7 4.6 %collective-permute-start.5 = (bf16[2,2,128,256]{3,2,1,0:T(8,128)(2,1)S(1)}, bf16[2,2,128,256]{3,2,1,0:T(8,128)(2,1)S(1)}, u32[]{:S(2)}, u32[]{:S(2)}) collective-permute-start(bf16[2,2,128,256]{3,2,1,0:T(8,128)(2,1)S(1)} %get-tuple-element.23), channel_id=1, source_target_pairs={{0,2},{1,3},{2,4},{3,5},{4,6},{5,7},{6,8},{7,9},{8,10},{9,11},{10,... | collective-permute-start | bytes 786440 | tf_op jit(solution)/shard_map/ppermute | solution.py:30
  39.2 4.2 %collective-permute-start.4 = (bf16[2,2,128,256]{3,2,1,0:T(8,128)(2,1)S(1)}, bf16[2,2,128,256]{3,2,1,0:T(8,128)(2,1)S(1)}, u32[]{:S(2)}, u32[]{:S(2)}) collective-permute-start(bf16[2,2,128,256]{3,2,1,0:T(8,128)(2,1)S(1)} %get-tuple-element.24), channel_id=1, source_target_pairs={{0,1},{1,2},{2,3},{3,4},{4,5},{5,6},{6,7},{7,8},{8,9},{9,10},{10,1... | collective-permute-start | bytes 786440 | tf_op jit(solution)/shard_map/ppermute | solution.py:30
  43.4 0.9 collective-permute-done.5.refs_1_
  45.2 5.2 %place.1.field = f32[2,2,128,2048]{3,2,1,0:T(8,128)} custom-call(s32[3,2,3]{2,1,0:T(2,128)} %pad_add_fusion.tables, f32[2,2,128,2048]{3,2,1,0:T(8,128)} %field.3, f32[2,2,128,256]{3,2,1,0:T(8,128)} %get-tuple-element.10.own, bf16[2,2,128,256]{3,2,1,0:T(8,128)(2,1)} %copy-done.1, bf16[2,2,128,256]{3,2,1,0:T(8,128)(2,1)} %copy-done), custom_call_target="tpu_custom_call" | custom-call | tf_op jit(solution)/shard_map/place/pallas_call | solution.py:460
  50.5 1.1 fusion
  51.5 1.3 %collective-permute-start.7 = (f32[2,2,1,2048]{3,2,1,0:T(1,128)S(1)}, f32[2,2,1,2048]{3,2,1,0:T(1,128)S(1)}, u32[]{:S(2)}, u32[]{:S(2)}) collective-permute-start(f32[2,2,1,2048]{3,2,1,0:T(1,128)S(1)} %get-tuple-element.18), channel_id=1, source_target_pairs={{1,0},{2,1},{3,2},{4,3},{5,4},{6,5},{7,6},{8,7},{9,8},{10,9},{11,1... | collective-permute-start | bytes 98312 | tf_op jit(solution)/shard_map/ppermute | solution.py:30
  52.8 7.0 %collective-permute-start.6 = (f32[2,2,1,2048]{3,2,1,0:T(1,128)S(1)}, f32[2,2,1,2048]{3,2,1,0:T(1,128)S(1)}, u32[]{:S(2)}, u32[]{:S(2)}) collective-permute-start(f32[2,2,1,2048]{3,2,1,0:T(1,128)S(1)} %get-tuple-element.19), channel_id=1, source_target_pairs={{0,1},{1,2},{2,3},{3,4},{4,5},{5,6},{6,7},{7,8},{8,9},{9,10},{10,1... | collective-permute-start | bytes 98312 | tf_op jit(solution)/shard_map/ppermute | solution.py:30
  59.8 5.4 %tables.1 = (bf16[1024,1024]{1,0:T(8,128)(2,1)}, bf16[1024,1024]{1,0:T(8,128)(2,1)}, bf16[1024,1024]{1,0:T(8,128)(2,1)}, bf16[1024,1024]{1,0:T(8,128)(2,1)}) custom-call(f32[2,4,32,1024]{3,2,1,0:T(8,128)} %constant.16.clone.factors), custom_call_target="tpu_custom_call" | custom-call | flops 10485760 | bytes 8388608 | tf_op jit(solution)/shard_map/tables/pallas_call | solution.py:432
  65.3 0.6 copy-done.4
  65.9 15.6 %forward.1 = (f32[2,128,2048]{2,1,0:T(8,128)}, f32[2,2,2048]{2,1,0:T(2,128)}) custom-call(f32[2,2,128,2048]{3,2,1,0:T(8,128)} %place.1.field, f32[2,2,1,2048]{3,2,1,0:T(1,128)} %copy-done.5, f32[2,2,1,2048]{3,2,1,0:T(1,128)} %copy-done.4, bf16[1024,1024]{1,0:T(8,128)(2,1)} %get-tuple-element.12.even_hi, bf16[1024,1024]{1,0:T(8,128)(2,1)} %get-tuple-element.13.even_lo, ...), custom_call_target="tpu_custom_call" | custom-call | tf_op jit(solution)/shard_map/forward/pallas_call | solution.py:471
  81.5 26.6 %all-gather = f32[32,2,2048]{2,1,0:T(2,128)} all-gather(f32[2,2,2048]{2,1,0:T(2,128)} %get-tuple-element.17), channel_id=2, replica_groups=mesh['group'=2,'tile'=16] {'tile'}, dimensions={0}, use_global_device_ids=true | all-gather | bytes 557056 | tf_op jit(solution)/shard_map/all_gather | solution.py:480
  108.1 11.5 %inverse.1 = f32[2,128,2048]{2,1,0:T(8,128)} custom-call(s32[1]{0:T(128)} %bitcast.8.place, f32[2,128,2048]{2,1,0:T(8,128)} %get-tuple-element.16.value, f32[16,2,2,2048]{3,2,1,0:T(2,128)} %bitcast.15, bf16[1024,1024]{1,0:T(8,128)(2,1)} %get-tuple-element.12.even_hi, bf16[1024,1024]{1,0:T(8,128)(2,1)} %get-tuple-element.13.even_lo, ...), custom_call_target="tpu_custom_call" | custom-call | tf_op jit(solution)/shard_map/inverse/pallas_call | solution.py:482
  (15 shorter events, 1.0 us)
Async XLA Ops:
  0.6 6.8 %collective-permute-start = (s32[2,3]{1,0:T(2,128)}, s32[2,3]{1,0:T(2,128)S(1)}, u32[]{:S(2)}, u32[]{:S(2)}) collective-permute-start(s32[2,3]{1,0:T(2,128)} %table.1), channel_id=1, source_target_pairs={{0,1},{1,2},{2,3},{3,4},{4,5},{5,6},{6,7},{7,8},{8,9},{9,10},{10,1... | collective-permute-start | bytes 80 | tf_op jit(solution)/shard_map/ppermute | solution.py:30
  3.0 5.9 %collective-permute-start.1 = (s32[2,3]{1,0:T(2,128)}, s32[2,3]{1,0:T(2,128)S(1)}, u32[]{:S(2)}, u32[]{:S(2)}) collective-permute-start(s32[2,3]{1,0:T(2,128)} %table.1), channel_id=1, source_target_pairs={{0,2},{1,3},{2,4},{3,5},{4,6},{5,7},{6,8},{7,9},{8,10},{9,11},{10,... | collective-permute-start | bytes 80 | tf_op jit(solution)/shard_map/ppermute | solution.py:30
  15.8 11.0 %collective-permute-start.3 = (bf16[2,2,128,256]{3,2,1,0:T(8,128)(2,1)S(1)}, bf16[2,2,128,256]{3,2,1,0:T(8,128)(2,1)S(1)}, u32[]{:S(2)}, u32[]{:S(2)}) collective-permute-start(bf16[2,2,128,256]{3,2,1,0:T(8,128)(2,1)S(1)} %get-tuple-element.20), channel_id=1, source_target_pairs={{2,0},{3,1},{4,2},{5,3},{6,4},{7,5},{8,6},{9,7},{10,8},{11,9},{12,... | collective-permute-start | bytes 786440 | tf_op jit(solution)/shard_map/ppermute | solution.py:30
  17.1 9.7 %collective-permute-start.2 = (bf16[2,2,128,256]{3,2,1,0:T(8,128)(2,1)S(1)}, bf16[2,2,128,256]{3,2,1,0:T(8,128)(2,1)S(1)}, u32[]{:S(2)}, u32[]{:S(2)}) collective-permute-start(bf16[2,2,128,256]{3,2,1,0:T(8,128)(2,1)S(1)} %get-tuple-element.21), channel_id=1, source_target_pairs={{1,0},{2,1},{3,2},{4,3},{5,4},{6,5},{7,6},{8,7},{9,8},{10,9},{11,1... | collective-permute-start | bytes 786440 | tf_op jit(solution)/shard_map/ppermute | solution.py:30
  26.8 0.7 copy-start.2
  26.8 0.8 copy-start.3
  34.7 9.7 %collective-permute-start.5 = (bf16[2,2,128,256]{3,2,1,0:T(8,128)(2,1)S(1)}, bf16[2,2,128,256]{3,2,1,0:T(8,128)(2,1)S(1)}, u32[]{:S(2)}, u32[]{:S(2)}) collective-permute-start(bf16[2,2,128,256]{3,2,1,0:T(8,128)(2,1)S(1)} %get-tuple-element.23), channel_id=1, source_target_pairs={{0,2},{1,3},{2,4},{3,5},{4,6},{5,7},{6,8},{7,9},{8,10},{9,11},{10,... | collective-permute-start | bytes 786440 | tf_op jit(solution)/shard_map/ppermute | solution.py:30
  39.2 5.3 %collective-permute-start.4 = (bf16[2,2,128,256]{3,2,1,0:T(8,128)(2,1)S(1)}, bf16[2,2,128,256]{3,2,1,0:T(8,128)(2,1)S(1)}, u32[]{:S(2)}, u32[]{:S(2)}) collective-permute-start(bf16[2,2,128,256]{3,2,1,0:T(8,128)(2,1)S(1)} %get-tuple-element.24), channel_id=1, source_target_pairs={{0,1},{1,2},{2,3},{3,4},{4,5},{5,6},{6,7},{7,8},{8,9},{9,10},{10,1... | collective-permute-start | bytes 786440 | tf_op jit(solution)/shard_map/ppermute | solution.py:30
  44.3 0.7 copy-start
  44.5 0.7 copy-start.1
  51.5 13.7 %collective-permute-start.7 = (f32[2,2,1,2048]{3,2,1,0:T(1,128)S(1)}, f32[2,2,1,2048]{3,2,1,0:T(1,128)S(1)}, u32[]{:S(2)}, u32[]{:S(2)}) collective-permute-start(f32[2,2,1,2048]{3,2,1,0:T(1,128)S(1)} %get-tuple-element.18), channel_id=1, source_target_pairs={{1,0},{2,1},{3,2},{4,3},{5,4},{6,5},{7,6},{8,7},{9,8},{10,9},{11,1... | collective-permute-start | bytes 98312 | tf_op jit(solution)/shard_map/ppermute | solution.py:30
  52.8 12.4 %collective-permute-start.6 = (f32[2,2,1,2048]{3,2,1,0:T(1,128)S(1)}, f32[2,2,1,2048]{3,2,1,0:T(1,128)S(1)}, u32[]{:S(2)}, u32[]{:S(2)}) collective-permute-start(f32[2,2,1,2048]{3,2,1,0:T(1,128)S(1)} %get-tuple-element.19), channel_id=1, source_target_pairs={{0,1},{1,2},{2,3},{3,4},{4,5},{5,6},{6,7},{7,8},{8,9},{9,10},{10,1... | collective-permute-start | bytes 98312 | tf_op jit(solution)/shard_map/ppermute | solution.py:30
  65.2 0.6 copy-start.4
  65.3 0.6 copy-start.5

commit v2 on v1

--- a/solution.py
+++ b/solution.py
@@ -18,20 +18,177 @@
 LANES = 128
 GROUP = 8
 TILE = 256
-VMEM_BYTES = 60 * 1024 * 1024
+VMEM_BYTES = 30 * 1024 * 1024
+MESH = pl.DeviceIdType.MESH
 vmem = pl.BlockSpec(memory_space=pltpu.VMEM)
 smem = pl.BlockSpec(memory_space=pltpu.SMEM)
 hbm = pl.BlockSpec(memory_space=pl.ANY)
 
 
-def passed_along(x, axis, by):
-    size = lax.axis_size(axis)
-    pairs = [(i, i + by) for i in range(size) if 0 <= i + by < size]
-    return lax.ppermute(x, axis, pairs)
-
-
 def params(**more):
     return pltpu.CompilerParams(vmem_limit_bytes=VMEM_BYTES, **more)
+
+
+def exchange_kernel(moves, keep, source, out, send_sems, recv_sems):
+    count = lax.axis_size("tile")
+    me = lax.axis_index("tile")
+    barrier = pltpu.get_barrier_semaphore()
+    met = jnp.zeros((), jnp.int32)
+    for by in sorted({sign * by for _, _, by in moves for sign in (1, -1)}):
+        there = (me + by >= 0) & (me + by < count)
+
+        @pl.when(there)
+        def _():
+            pl.semaphore_signal(
+                barrier, inc=1, device_id={"tile": me + by}, device_id_type=MESH
+            )
+
+        met = met + jnp.where(there, 1, 0)
+    pl.semaphore_wait(barrier, met)
+    copies = []
+    for index, (first, last, by) in enumerate(moves):
+        copy = pltpu.make_async_remote_copy(
+            src_ref=source.at[first],
+            dst_ref=out.at[last],
+            send_sem=send_sems.at[index],
+            recv_sem=recv_sems.at[index],
+            device_id={"tile": me + by},
+            device_id_type=MESH,
+        )
+        sends = (me + by >= 0) & (me + by < count)
+        takes = (me - by >= 0) & (me - by < count)
+        copies.append((copy, sends, takes, last))
+        pl.when(sends)(copy.start)
+    for first, last in keep:
+        out[last] = source[first]
+    for copy, sends, takes, last in copies:
+
+        @pl.when(jnp.logical_not(takes))
+        def _():
+            out[last] = jnp.zeros(out.shape[1:], out.dtype)
+
+    for copy, sends, takes, last in copies:
+        pl.when(takes)(copy.wait_recv)
+        pl.when(sends)(copy.wait_send)
+
+
+def exchanged(source, slots, moves, keep, number, name):
+    return pl.pallas_call(
+        functools.partial(exchange_kernel, moves, keep),
+        out_shape=jax.ShapeDtypeStruct((slots,) + source.shape[1:], source.dtype),
+        in_specs=[vmem],
+        out_specs=vmem,
+        scratch_shapes=[pltpu.SemaphoreType.DMA((len(moves),))] * 2,
+        compiler_params=params(collective_id=number, has_side_effects=True),
+        name=name,
+    )(source)
+
+
+def join_kernel(ends, powers, extra, out, heard, told, up_sems, in_sems, down_sems, back_sems):
+    count = lax.axis_size("tile")
+    me = lax.axis_index("tile")
+    blocks, lines = ends.shape[0], ends.shape[1]
+    angles = lines // 2
+    stride = count // blocks
+    mine = me // stride
+    joins = lax.rem(me, stride) == 0
+    barrier = pltpu.get_barrier_semaphore()
+
+    def greet(by, _):
+        pl.semaphore_signal(
+            barrier, inc=1, device_id={"tile": lax.rem(me + by, count)}, device_id_type=MESH
+        )
+        return 0
+
+    lax.fori_loop(1, count, greet, 0)
+    pl.semaphore_wait(barrier, count - 1)
+
+    def up(by):
+        block = lax.rem(mine + by, blocks)
+        return pltpu.make_async_remote_copy(
+            src_ref=ends.at[block],
+            dst_ref=heard.at[me],
+            send_sem=up_sems.at[block],
+            recv_sem=in_sems.at[me],
+            device_id={"tile": block * stride},
+            device_id_type=MESH,
+        )
+
+    def came(other):
+        return pltpu.make_async_remote_copy(
+            src_ref=ends.at[0],
+            dst_ref=heard.at[other],
+            send_sem=up_sems.at[0],
+            recv_sem=in_sems.at[other],
+            device_id={"tile": other},
+            device_id_type=MESH,
+        )
+
+    def down(other):
+        return pltpu.make_async_remote_copy(
+            src_ref=told.at[other],
+            dst_ref=out.at[mine],
+            send_sem=down_sems.at[other],
+            recv_sem=back_sems.at[mine],
+            device_id={"tile": other},
+            device_id_type=MESH,
+        )
+
+    def answered(block):
+        return pltpu.make_async_remote_copy(
+            src_ref=told.at[0],
+            dst_ref=out.at[block],
+            send_sem=down_sems.at[0],
+            recv_sem=back_sems.at[block],
+            device_id={"tile": block * stride},
+            device_id_type=MESH,
+        )
+
+    def each(limit, step):
+        def run(index, _):
+            step(index)
+            return 0
+
+        lax.fori_loop(0, limit, run, 0)
+
+    for by in range(blocks):
+        pl.when(lax.rem(mine + by, blocks) * stride != me)(lambda: up(by).start())
+
+    @pl.when(joins)
+    def _():
+        heard[me] = ends[mine]
+        for by in range(1, count):
+            came(lax.rem(me + by, count)).wait_recv()
+        step = powers[mine, 1:2]
+        whole = powers[mine, count : count + 1]
+        closing = extra[mine, 1:2]
+        gain = extra[mine, 0:1]
+        wall = heard[count - 1, angles:]
+        floor = heard[0, :angles]
+        for strip in range(1, count):
+            floor = floor * step + heard[strip, :angles]
+            wall = wall * step + heard[count - 1 - strip, angles:]
+        enter = (wall + whole * floor) * closing
+        leave = (floor + whole * wall) * closing
+        for strip in range(count):
+            told[strip, :angles] = enter * gain
+            enter = enter * step + heard[strip, :angles]
+            back = count - 1 - strip
+            told[back, angles:] = leave * gain
+            leave = leave * step + heard[back, angles:]
+        for by in range(1, count):
+            down(lax.rem(me + by, count)).start()
+        out[mine] = told[me]
+
+    for by in range(blocks):
+        block = lax.rem(mine + by, blocks)
+        pl.when(block * stride != me)(lambda: answered(block).wait_recv())
+        pl.when(block * stride != me)(lambda: up(by).wait_send())
+
+    @pl.when(joins)
+    def _():
+        for by in range(1, count):
+            down(lax.rem(me + by, count)).wait_send()
 
 
 def fourier_tables(side):
@@ -86,7 +243,7 @@
         [gain, 1.0 / (1.0 - np.exp(-2.0 * grid_side * rate)), np.exp(-GROUP * rate)]
         + [rate * 0.0] * 5
     )
-    return jnp.asarray(local, f32), jnp.asarray(powers, f32), jnp.asarray(extra, f32)
+    return local.astype(np.float32), powers.astype(np.float32), extra.astype(np.float32)
 
 
 def table_kernel(factors, even_hi, even_lo, odd_hi, odd_lo):
@@ -134,9 +291,10 @@
             out[j, s, part] = turned[:, :side].astype(bf16)
 
 
-def frame_kernel(table, counts, probe, measured, cos_ref, sin_ref, *refs):
-    pieces = refs[: len(refs) - 3]
-    own_out, away_out, window = refs[len(refs) - 3 :]
+def frame_kernel(
+    table, counts, probe, measured, cos_ref, sin_ref, cuts, arrived, own_out, away_out, window
+):
+    pieces = [cuts.at[0]] + [arrived.at[j] for j in range(arrived.shape[0])]
     cap, side = measured.shape[0], measured.shape[1]
     strip = pieces[0].shape[2]
     reach = len(pieces) - 1
@@ -195,8 +353,8 @@
                 away_out[j - 1, s, part] = turned[j * strip : (j + 1) * strip].astype(bf16)
 
 
-def place_kernel(tables, field, own, *refs):
-    away, out = refs[:-1], refs[-1]
+def place_kernel(tables, field, own, away_ref, out, edges):
+    away = [away_ref.at[j] for j in range(away_ref.shape[0])]
     width = field.shape[3]
     cap, side = own.shape[0], own.shape[3]
     span = side + LANES
@@ -214,6 +372,11 @@
                 out[angle, part, :, pl.ds(start, span)] = (
                     out[angle, part, :, pl.ds(start, span)] + turned
                 )
+    strip = field.shape[2]
+    for angle in range(field.shape[0]):
+        for part in range(2):
+            edges[0, angle, part] = out[angle, part, :1]
+            edges[1, angle, part] = out[angle, part, strip - 1 :]
 
 
 def mirror(value):
@@ -243,7 +406,7 @@
 
 
 def forward_kernel(
-    field, above, below, even_hi, even_lo, odd_hi, odd_lo, local, extra,
+    field, halo, even_hi, even_lo, odd_hi, odd_lo, local, extra,
     out, ends, source, xeh, xel, xoh, xol,
 ):
     angles, _, strip, width = field.shape
@@ -256,12 +419,12 @@
             for part in range(2):
                 body = field[angle, part, first : first + block]
                 before = (
-                    above[angle, part]
+                    halo[0, angle, part]
                     if first == 0
                     else field[angle, part, first - 1 : first]
                 )
                 after = (
-                    below[angle, part]
+                    halo[1, angle, part]
                     if first + block == strip
                     else field[angle, part, first + block : first + block + 1]
                 )
@@ -313,7 +476,7 @@
                     item = item + local[3, :, where] * carry
                 carry = item[GROUP - 1 :]
                 falls.append(item)
-            ends[0, angle : angle + 1, where] = carry
+            ends[first // LANES, angle : angle + 1] = carry
             rises, carry = [None] * groups, None
             for group in reversed(range(groups)):
                 item = rise[group]
@@ -321,7 +484,7 @@
                     item = item + local[7, :, where] * carry
                 carry = item[:1]
                 rises[group] = item
-            ends[1, angle : angle + 1, where] = carry
+            ends[first // LANES, angles + angle : angles + angle + 1] = carry
             for group in range(groups):
                 out[angle, group * GROUP : (group + 1) * GROUP, where] = gain * (
                     falls[group] + rises[group] - value[group]
@@ -329,38 +492,16 @@
 
 
 def inverse_kernel(
-    place, value, ends, even_hi, even_lo, odd_hi, odd_lo, local, powers, extra,
-    out, incoming, xh, xl,
+    value, incoming, even_hi, even_lo, odd_hi, odd_lo, local, extra, out, xh, xl
 ):
     angles, strip, width = value.shape
     half = width // 2
-    strips = ends.shape[0]
-    me = place[0]
-    wall = jnp.zeros((angles, width), f32)
-    floor = jnp.zeros((angles, width), f32)
-    enter = jnp.zeros((angles, width), f32)
-    leave = jnp.zeros((angles, width), f32)
-    for b in range(strips):
-        right_end, left_end = ends[b, 0], ends[b, 1]
-        wall = wall + powers[b : b + 1] * left_end
-        floor = floor + powers[strips - 1 - b : strips - b] * right_end
-        weight = powers[pl.ds(jnp.maximum(me - 1 - b, 0), 1)]
-        enter = enter + jnp.where(b < me, weight, 0.0) * right_end
-        weight = powers[pl.ds(jnp.maximum(b - me - 1, 0), 1)]
-        leave = leave + jnp.where(b > me, weight, 0.0) * left_end
-    whole = powers[strips : strips + 1]
-    closing = extra[1:2]
-    gain = extra[0:1]
-    enter = enter + powers[pl.ds(me, 1)] * (wall + whole * floor) * closing
-    leave = leave + powers[pl.ds(strips - 1 - me, 1)] * (floor + whole * wall) * closing
-    incoming[0] = enter * gain
-    incoming[1] = leave * gain
     groups = strip // GROUP
     for first in range(0, width, LANES):
         where = slice(first, first + LANES)
         for angle in range(angles):
-            fall = incoming[0, angle : angle + 1, where]
-            rise = incoming[1, angle : angle + 1, where]
+            fall = incoming[first // LANES, angle : angle + 1]
+            rise = incoming[first // LANES, angles + angle : angles + angle + 1]
             step = extra[2:3, where]
             falls, rises = [], []
             for group in range(groups):
@@ -408,12 +549,13 @@
     half = width // 2
     reach = side // strip
     rows = angles * strip
+    strips = lax.axis_size("tile")
+    blocks = width // LANES
     shape = jax.ShapeDtypeStruct
 
-    above_tables = [frame_table] + [
-        passed_along(frame_table, "tile", j) for j in range(1, reach + 1)
-    ]
-    tables = jnp.stack(above_tables)
+    tables = exchanged(
+        frame_table[None], reach + 1, [(0, j, j) for j in range(1, reach + 1)], [(0, 0)], 0, "tell"
+    )
     cuts = pl.pallas_call(
         cut_kernel,
         out_shape=shape((reach + 1, cap, 2, strip, side), bf16),
@@ -426,7 +568,7 @@
         compiler_params=params(),
         name="cut",
     )(tables, object_field)
-    pieces = [cuts[0]] + [passed_along(cuts[j], "tile", -j) for j in range(1, reach + 1)]
+    arrived = exchanged(cuts, reach, [(j, j - 1, -j) for j in range(1, reach + 1)], [], 1, "fetch")
 
     factors = cosine_factors(width)
     half_tables = pl.pallas_call(
@@ -441,6 +583,10 @@
         name="tables",
     )(factors)
     local, powers, extra = decay_tables(width, strip)
+
+    def by_block(table):
+        return jnp.asarray(table.reshape(-1, blocks, LANES).transpose(1, 0, 2))
+
     cos_part, sin_part = fourier_tables(side)
 
     own, away = pl.pallas_call(
@@ -449,49 +595,61 @@
             shape((cap, 2, strip, side), f32),
             shape((reach, cap, 2, strip, side), bf16),
         ],
-        in_specs=[smem, smem] + [vmem] * (5 + reach),
+        in_specs=[smem, smem] + [vmem] * 6,
         out_specs=[vmem, vmem],
         scratch_shapes=[pltpu.VMEM(((reach + 1) * strip, side), f32)],
         compiler_params=params(),
         name="frames",
-    )(frame_table, frame_count, probe, measured, cos_part, sin_part, *pieces)
-    arrived = [passed_along(away[j - 1], "tile", j) for j in range(1, reach + 1)]
-
-    updated = pl.pallas_call(
+    )(frame_table, frame_count, probe, measured, cos_part, sin_part, cuts, arrived)
+    landed = exchanged(away, reach, [(j - 1, j - 1, j) for j in range(1, reach + 1)], [], 2, "give")
+
+    updated, edges = pl.pallas_call(
         place_kernel,
-        out_shape=shape(object_field.shape, f32),
-        in_specs=[smem, vmem, vmem] + [vmem] * reach,
-        out_specs=vmem,
+        out_shape=[shape(object_field.shape, f32), shape((2, angles, 2, 1, width), f32)],
+        in_specs=[smem, vmem, vmem, vmem],
+        out_specs=[vmem, vmem],
         compiler_params=params(),
         name="place",
-    )(tables, object_field, own, *arrived)
-    above = passed_along(updated[:, :, strip - 1 :], "tile", 1)
-    below = passed_along(updated[:, :, :1], "tile", -1)
+    )(tables, object_field, own, landed)
+    halo = exchanged(edges, 2, [(1, 0, 1), (0, 1, -1)], [], 3, "edges")
 
     solved, ends = pl.pallas_call(
         forward_kernel,
-        out_shape=[shape((angles, strip, width), f32), shape((2, angles, width), f32)],
-        in_specs=[vmem] * 9,
+        out_shape=[shape((angles, strip, width), f32), shape((blocks, 2 * angles, LANES), f32)],
+        in_specs=[vmem] * 8,
         out_specs=[vmem, vmem],
         scratch_shapes=[pltpu.VMEM((rows, width), f32)] + [pltpu.VMEM((rows, half), bf16)] * 4,
         compiler_params=params(),
         name="forward",
-    )(updated, above, below, *half_tables, local, extra)
-    every_end = lax.all_gather(ends, "tile")
-    place = lax.axis_index("tile").astype(jnp.int32).reshape(1)
+    )(updated, halo, *half_tables, local, extra)
+    incoming = pl.pallas_call(
+        join_kernel,
+        out_shape=shape(ends.shape, f32),
+        in_specs=[vmem] * 3,
+        out_specs=vmem,
+        scratch_shapes=[
+            pltpu.VMEM((strips, 2 * angles, LANES), f32),
+            pltpu.VMEM((strips, 2 * angles, LANES), f32),
+            pltpu.SemaphoreType.DMA((blocks,)),
+            pltpu.SemaphoreType.DMA((strips,)),
+            pltpu.SemaphoreType.DMA((strips,)),
+            pltpu.SemaphoreType.DMA((blocks,)),
+        ],
+        compiler_params=params(collective_id=4, has_side_effects=True),
+        name="join",
+    )(ends, by_block(powers), by_block(extra))
     phase_map = pl.pallas_call(
         inverse_kernel,
         out_shape=shape((angles, strip, width), f32),
-        in_specs=[smem] + [vmem] * 9,
+        in_specs=[vmem] * 8,
         out_specs=vmem,
         scratch_shapes=[
-            pltpu.VMEM((2, angles, width), f32),
             pltpu.VMEM((rows, width), bf16),
             pltpu.VMEM((rows, width), bf16),
         ],
         compiler_params=params(),
         name="inverse",
-    )(place, solved, every_end, *half_tables, local, powers, extra)
+    )(solved, incoming, *half_tables, local, extra)
     return (updated, phase_map)
 
 

time: 120 us -> 79.8 us (0.66)
  blocking collectives: 26.6 us -> 0 us
  starting transfers between devices: 26.4 us -> 0 us
  Pallas kernels: 47.5 us -> 73 us
  waiting for transfers between devices: 10.4 us -> 0 us
  other arithmetic: 1.27 us -> 0 us
    pallas_call x1 -> x6, Pallas kernels: 5.22 us -> 48.8 us  [the longest x4 29.2 us: exchanged(): pl.pallas_call(functools.partial(exchange_kernel, moves, keep), out_shape...]
    all_gather x1 -> x0, blocking collectives: 26.6 us -> none  [body(): every_end = lax.all_gather(ends, 'tile')]
    ppermute x8 -> x0, starting transfers between devices: 26.4 us -> none  [passed_along(): return lax.ppermute(x, axis, pairs)]
    ppermute x8 -> x0, waiting for transfers between devices: 10.4 us -> none  [passed_along(): return lax.ppermute(x, axis, pairs)]
    pallas_call x1, Pallas kernels: 15.6 us -> 9.35 us  [body(): pl.pallas_call(forward_kernel, out_shape=[shape((angles, strip, width), f...]
    pallas_call x1, Pallas kernels: 11.5 us -> 6.63 us  [body(): pl.pallas_call(inverse_kernel, out_shape=shape((angles, strip, width), f3...]
    pallas_call x1, Pallas kernels: 5.41 us -> 2.05 us  [body(): pl.pallas_call(table_kernel, out_shape=[shape((half, half), bf16)] * 4, i...]
    unnamed x12 -> x26, local copies, waits for them, and re-layouts: 2.08 us -> 5.09 us
  transfers between devices with their start and end apart: 8 -> 0, of which waited for: 4 -> 0; matrix products, arithmetic and copies ran while one was open for 0% -> 0% of each run, Pallas kernels for 5% -> 0%
where the time goes in v2:
time: 79.8 us; the launch traced here: 79.6 us
  Pallas kernels  73 us (91%)
  local copies, waits for them, and re-layouts  5.09 us (6%)
  between operations  1.49 us (2%)
    pallas_call x4, Pallas kernels, exchanged(): pl.pallas_call(functools.partial(exchange_kernel, moves, keep), out_shape...  29.2 us
    pallas_call x1, Pallas kernels, body(): pl.pallas_call(join_kernel, out_shape=shape(ends.shape, f32), in_specs=[v...  16.2 us
    pallas_call x1, Pallas kernels, body(): pl.pallas_call(forward_kernel, out_shape=[shape((angles, strip, width), f...  9.35 us
    pallas_call x1, Pallas kernels, body(): pl.pallas_call(inverse_kernel, out_shape=shape((angles, strip, width), f3...  6.63 us
    unnamed x26, local copies, waits for them, and re-layouts  5.09 us
    pallas_call x1, Pallas kernels, body(): pl.pallas_call(frame_kernel, out_shape=[shape((cap, 2, strip, side), f32)...  4.3 us
    pallas_call x1, Pallas kernels, body(): pl.pallas_call(place_kernel, out_shape=[shape(object_field.shape, f32), s...  3.36 us
    pallas_call x1, Pallas kernels, body(): pl.pallas_call(table_kernel, out_shape=[shape((half, half), bf16)] * 4, i...  2.05 us

profile of v2, /device:TPU:0, one launch (start us, length us, event | category | flops | bytes accessed | tf_op | source)
XLA Modules:
  0.0 79.6 jit_solution(5719702552093264719)
XLA Ops:
  1.3 0.0 copy-start.12
  1.3 0.7 copy-done.12
  2.0 4.3 %tell.1.tables = s32[3,2,3]{2,1,0:T(2,128)S(1)} custom-call(s32[1,2,3]{2,1,0:T(2,128)S(1)} %bitcast.1), custom_call_target="tpu_custom_call" | custom-call | tf_op jit(solution)/shard_map/tell/pallas_call | solution.py:76
  6.3 0.0 copy-start
  6.3 2.2 %copy-done = f32[2,2,128,2048]{3,2,1,0:T(8,128)S(1)} copy-done((f32[2,2,128,2048]{3,2,1,0:T(8,128)S(1)}, f32[2,2,128,2048]{3,2,1,0:T(8,128)}, u32[]{:S(2)}) %copy-start) | copy-done | bytes 4194328
  8.5 1.9 %cut.1.source.cuts = bf16[3,2,2,128,256]{4,3,2,1,0:T(8,128)(2,1)S(1)} custom-call(s32[3,2,3]{2,1,0:T(2,128)S(1)} %tell.1.tables, f32[2,2,128,2048]{3,2,1,0:T(8,128)S(1)} %copy-done), custom_call_target="tpu_custom_call" | custom-call | tf_op jit(solution)/shard_map/cut/pallas_call | solution.py:559
  10.4 0.0 copy-start.1
  10.4 14.2 %fetch.1.arrived = bf16[2,2,2,128,256]{4,3,2,1,0:T(8,128)(2,1)S(1)} custom-call(bf16[3,2,2,128,256]{4,3,2,1,0:T(8,128)(2,1)S(1)} %cut.1.source.cuts), custom_call_target="tpu_custom_call" | custom-call | tf_op jit(solution)/shard_map/fetch/pallas_call | solution.py:76
  24.6 0.0 copy-done.5
  24.6 4.3 %frames.1 = (f32[2,2,128,256]{3,2,1,0:T(8,128)S(1)}, bf16[2,2,2,128,256]{4,3,2,1,0:T(8,128)(2,1)S(1)}) custom-call(s32[2,3]{1,0:T(2,128)S(1)} %copy-done.12, s32[1]{0:T(128)S(6)} %copy.14.counts, f32[2,256,256]{2,1,0:T(8,128)S(1)} %copy-done.5, bf16[2,256,256]{2,1,0:T(8,128)(2,1)S(1)} %copy-done.7, bf16[256,256]{1,0:T(8,128)(2,1)S(1)} %copy-done.10, ...), custom_call_target="tpu_custom_call" | custom-call | tf_op jit(solution)/shard_map/frames/pallas_call | solution.py:592
  28.9 7.4 %give.1.away_ref = bf16[2,2,2,128,256]{4,3,2,1,0:T(8,128)(2,1)S(1)} custom-call(bf16[2,2,2,128,256]{4,3,2,1,0:T(8,128)(2,1)S(1)} %get-tuple-element.13.source), custom_call_target="tpu_custom_call" | custom-call | tf_op jit(solution)/shard_map/give/pallas_call | solution.py:76
  36.3 0.0 copy-done.1
  36.3 0.0 copy-start.4
  36.3 0.0 copy-start.3
  36.4 0.0 copy-start.6
  36.4 3.4 %place.1 = (f32[2,2,128,2048]{3,2,1,0:T(8,128)}, f32[2,2,2,1,2048]{4,3,2,1,0:T(1,128)S(1)}) custom-call(s32[3,2,3]{2,1,0:T(2,128)S(1)} %tell.1.tables, f32[2,2,128,2048]{3,2,1,0:T(8,128)S(1)} %copy-done.1, f32[2,2,128,256]{3,2,1,0:T(8,128)S(1)} %get-tuple-element.12.own, bf16[2,2,2,128,256]{4,3,2,1,0:T(8,128)(2,1)S(1)} %give.1.away_ref), custom_call_target="tpu_custom_call" | custom-call | tf_op jit(solution)/shard_map/place/pallas_call | solution.py:606
  39.7 3.3 %edges.1.halo = f32[2,2,2,1,2048]{4,3,2,1,0:T(1,128)S(1)} custom-call(f32[2,2,2,1,2048]{4,3,2,1,0:T(1,128)S(1)} %get-tuple-element.15.source), custom_call_target="tpu_custom_call" | custom-call | tf_op jit(solution)/shard_map/edges/pallas_call | solution.py:76
  43.1 0.0 copy-done.4
  43.1 2.1 %tables.1 = (bf16[1024,1024]{1,0:T(8,128)(2,1)S(1)}, bf16[1024,1024]{1,0:T(8,128)(2,1)S(1)}, bf16[1024,1024]{1,0:T(8,128)(2,1)S(1)}, bf16[1024,1024]{1,0:T(8,128)(2,1)S(1)}) custom-call(f32[2,4,32,1024]{3,2,1,0:T(8,128)S(1)} %copy-done.4), custom_call_target="tpu_custom_call" | custom-call | flops 10485760 | bytes 8388608 | tf_op jit(solution)/shard_map/tables/pallas_call | solution.py:574
  45.2 0.0 copy-start.2
  45.2 2.2 %copy-done.2 = f32[2,2,128,2048]{3,2,1,0:T(8,128)S(1)} copy-done((f32[2,2,128,2048]{3,2,1,0:T(8,128)S(1)}, f32[2,2,128,2048]{3,2,1,0:T(8,128)}, u32[]{:S(2)}) %copy-start.2) | copy-done | bytes 4194328
  47.4 9.3 %forward.1 = (f32[2,128,2048]{2,1,0:T(8,128)S(1)}, f32[16,4,128]{2,1,0:T(4,128)S(1)}) custom-call(f32[2,2,128,2048]{3,2,1,0:T(8,128)S(1)} %copy-done.2, f32[2,2,2,1,2048]{4,3,2,1,0:T(1,128)S(1)} %edges.1.halo, bf16[1024,1024]{1,0:T(8,128)(2,1)S(1)} %get-tuple-element.16.even_hi, bf16[1024,1024]{1,0:T(8,128)(2,1)S(1)} %get-tuple-element.17.even_lo, ...), custom_call_target="tpu_custom_call" | custom-call | tf_op jit(solution)/shard_map/forward/pallas_call | solution.py:616
  56.7 16.2 %join.1.incoming = f32[16,4,128]{2,1,0:T(4,128)S(1)} custom-call(f32[16,4,128]{2,1,0:T(4,128)S(1)} %get-tuple-element.21.ends, f32[16,17,128]{2,1,0:T(8,128)S(1)} %copy-done.8, f32[16,8,128]{2,1,0:T(8,128)S(1)} %copy-done.11), custom_call_target="tpu_custom_call" | custom-call | tf_op jit(solution)/shard_map/join/pallas_call | solution.py:625
  73.0 6.6 %inverse.1 = f32[2,128,2048]{2,1,0:T(8,128)} custom-call(f32[2,128,2048]{2,1,0:T(8,128)S(1)} %get-tuple-element.20.value, f32[16,4,128]{2,1,0:T(4,128)S(1)} %join.1.incoming, bf16[1024,1024]{1,0:T(8,128)(2,1)S(1)} %get-tuple-element.16.even_hi, bf16[1024,1024]{1,0:T(8,128)(2,1)S(1)} %get-tuple-element.17.even_lo, ...), custom_call_target="tpu_custom_call" | custom-call | tf_op jit(solution)/shard_map/inverse/pallas_call | solution.py:641
  (13 shorter events, 0.0 us)
Async XLA Ops:
  1.3 0.7 copy-start.12
  6.3 2.2 %copy-start = (f32[2,2,128,2048]{3,2,1,0:T(8,128)S(1)}, f32[2,2,128,2048]{3,2,1,0:T(8,128)}, u32[]{:S(2)}) copy-start(f32[2,2,128,2048]{3,2,1,0:T(8,128)} %field.3) | copy-start | bytes 12582916
  8.5 16.1 %copy-start.5 = (f32[2,256,256]{2,1,0:T(8,128)S(1)}, f32[2,256,256]{2,1,0:T(8,128)}, u32[]{:S(2)}) copy-start(f32[2,256,256]{2,1,0:T(8,128)} %probe.1) | copy-start | bytes 1572868
  8.5 16.1 %copy-start.7 = (bf16[2,256,256]{2,1,0:T(8,128)(2,1)S(1)}, bf16[2,256,256]{2,1,0:T(8,128)(2,1)}, u32[]{:S(2)}) copy-start(bf16[2,256,256]{2,1,0:T(8,128)(2,1)} %measured.1) | copy-start | bytes 786436
  8.5 16.1 %copy-start.9 = (bf16[256,256]{1,0:T(8,128)(2,1)S(1)}, bf16[256,256]{1,0:T(8,128)(2,1)}, u32[]{:S(2)}) copy-start(bf16[256,256]{1,0:T(8,128)(2,1)} %constant.25.sin_ref) | copy-start | bytes 393220
  8.5 16.1 %copy-start.10 = (bf16[256,256]{1,0:T(8,128)(2,1)S(1)}, bf16[256,256]{1,0:T(8,128)(2,1)}, u32[]{:S(2)}) copy-start(bf16[256,256]{1,0:T(8,128)(2,1)} %constant.24.cos_ref) | copy-start | bytes 393220
  10.4 25.9 %copy-start.1 = (f32[2,2,128,2048]{3,2,1,0:T(8,128)S(1)}, f32[2,2,128,2048]{3,2,1,0:T(8,128)}, u32[]{:S(2)}) copy-start(f32[2,2,128,2048]{3,2,1,0:T(8,128)} %field.3) | copy-start | bytes 12582916
  36.3 6.7 %copy-start.4 = (f32[2,4,32,1024]{3,2,1,0:T(8,128)S(1)}, f32[2,4,32,1024]{3,2,1,0:T(8,128)}, u32[]{:S(2)}) copy-start(f32[2,4,32,1024]{3,2,1,0:T(8,128)} %constant.14.clone.factors) | copy-start | bytes 3145732
  36.3 8.8 %copy-start.3 = (f32[8,8,2048]{2,1,0:T(8,128)S(1)}, f32[8,8,2048]{2,1,0:T(8,128)}, u32[]{:S(2)}) copy-start(f32[8,8,2048]{2,1,0:T(8,128)} %constant.17.clone.local) | copy-start | bytes 1572868
  36.4 8.8 %copy-start.6 = (f32[8,2048]{1,0:T(8,128)S(1)}, f32[8,2048]{1,0:T(8,128)}, u32[]{:S(2)}) copy-start(f32[8,2048]{1,0:T(8,128)} %constant.18.clone.extra) | copy-start | bytes 196612
  45.2 2.2 %copy-start.2 = (f32[2,2,128,2048]{3,2,1,0:T(8,128)S(1)}, f32[2,2,128,2048]{3,2,1,0:T(8,128)}, u32[]{:S(2)}) copy-start(f32[2,2,128,2048]{3,2,1,0:T(8,128)} %get-tuple-element.10.field) | copy-start | bytes 12582916
  47.3 9.4 %copy-start.8 = (f32[16,17,128]{2,1,0:T(8,128)S(1)}, f32[16,17,128]{2,1,0:T(8,128)}, u32[]{:S(2)}) copy-start(f32[16,17,128]{2,1,0:T(8,128)} %constant.19.clone.powers) | copy-start | bytes 417796
  47.3 9.4 %copy-start.11 = (f32[16,8,128]{2,1,0:T(8,128)S(1)}, f32[16,8,128]{2,1,0:T(8,128)}, u32[]{:S(2)}) copy-start(f32[16,8,128]{2,1,0:T(8,128)} %constant.20.clone.extra) | copy-start | bytes 196612

commit v3 on v2

--- a/solution.py
+++ b/solution.py
@@ -22,7 +22,13 @@
 MESH = pl.DeviceIdType.MESH
 vmem = pl.BlockSpec(memory_space=pltpu.VMEM)
 smem = pl.BlockSpec(memory_space=pltpu.SMEM)
-hbm = pl.BlockSpec(memory_space=pl.ANY)
+hbm = pl.BlockSpec(memory_space=pltpu.HBM)
+
+
+def cost(micros):
+    return pl.CostEstimate(
+        flops=0, bytes_accessed=int(micros * 3_000_000), transcendentals=0
+    )
 
 
 def params(**more):
@@ -80,6 +86,7 @@
         out_specs=vmem,
         scratch_shapes=[pltpu.SemaphoreType.DMA((len(moves),))] * 2,
         compiler_params=params(collective_id=number, has_side_effects=True),
+        cost_estimate=cost(4),
         name=name,
     )(source)
 
@@ -353,7 +360,7 @@
                 away_out[j - 1, s, part] = turned[j * strip : (j + 1) * strip].astype(bf16)
 
 
-def place_kernel(tables, field, own, away_ref, out, edges):
+def place_kernel(tables, field, own, away_ref, updated, out, edges, sem):
     away = [away_ref.at[j] for j in range(away_ref.shape[0])]
     width = field.shape[3]
     cap, side = own.shape[0], own.shape[3]
@@ -377,6 +384,9 @@
         for part in range(2):
             edges[0, angle, part] = out[angle, part, :1]
             edges[1, angle, part] = out[angle, part, strip - 1 :]
+    copy = pltpu.make_async_copy(out, updated, sem)
+    copy.start()
+    copy.wait()
 
 
 def mirror(value):
@@ -413,34 +423,37 @@
     half = width // 2
     block = GROUP * 2
     columns = lax.broadcasted_iota(jnp.int32, (block, width), 1)
-    for angle in range(angles):
-        for first in range(0, strip, block):
-            here, up, down, left = [], [], [], []
-            for part in range(2):
-                body = field[angle, part, first : first + block]
-                before = (
-                    halo[0, angle, part]
-                    if first == 0
-                    else field[angle, part, first - 1 : first]
-                )
-                after = (
-                    halo[1, angle, part]
-                    if first + block == strip
-                    else field[angle, part, first + block : first + block + 1]
-                )
-                here.append(body)
-                up.append(jnp.concatenate([before, body[:-1]], 0))
-                down.append(jnp.concatenate([body[1:], after], 0))
-                left.append(jnp.where(columns == 0, 0.0, pltpu.roll(body, 1, 1)))
-            row_up = bond(*up, *here)
-            row_down = bond(*here, *down)
-            col_left = bond(*left, *here)
-            col_right = jnp.where(
-                columns == width - 1, 0.0, pltpu.roll(col_left, width - 1, 1)
+    blocks = strip // block
+
+    def gradients(index, _):
+        angle = index // blocks
+        first = pl.multiple_of(lax.rem(index, blocks) * block, block)
+        here, up, down, left = [], [], [], []
+        for part in range(2):
+            body = field[angle, part, pl.ds(first, block)]
+            before = jnp.where(
+                first == 0,
+                halo[0, angle, part],
+                field[angle, part, pl.ds(jnp.maximum(first - 1, 0), 1)],
             )
-            source[angle * strip + first : angle * strip + first + block] = -(
-                row_down - row_up + col_right - col_left
+            after = jnp.where(
+                first + block == strip,
+                halo[1, angle, part],
+                field[angle, part, pl.ds(jnp.minimum(first + block, strip - 1), 1)],
             )
+            here.append(body)
+            up.append(jnp.concatenate([before, body[:-1]], 0))
+            down.append(jnp.concatenate([body[1:], after], 0))
+            left.append(jnp.where(columns == 0, 0.0, pltpu.roll(body, 1, 1)))
+        row_up = bond(*up, *here)
+        row_down = bond(*here, *down)
+        col_left = bond(*left, *here)
+        col_right = jnp.where(columns == width - 1, 0.0, pltpu.roll(col_left, width - 1, 1))
+        start = pl.multiple_of(angle * strip + first, block)
+        source[pl.ds(start, block)] = -(row_down - row_up + col_right - col_left)
+        return 0
+
+    lax.fori_loop(0, angles * blocks, gradients, 0)
     for first in range(0, half, TILE):
         near = source[:, first : first + TILE]
         far = mirror(source[:, width - first - TILE : width - first])
@@ -459,8 +472,9 @@
                 + jnp.dot(high[...], table_lo[:, where], preferred_element_type=f32)
             )
     groups = strip // GROUP
-    for first in range(0, width, LANES):
-        where = slice(first, first + LANES)
+
+    def scan(chunk, _):
+        where = pl.ds(pl.multiple_of(chunk * LANES, LANES), LANES)
         gain = extra[0:1, where]
         for angle in range(angles):
             value = source[angle * strip : (angle + 1) * strip, where]
@@ -476,7 +490,7 @@
                     item = item + local[3, :, where] * carry
                 carry = item[GROUP - 1 :]
                 falls.append(item)
-            ends[first // LANES, angle : angle + 1] = carry
+            ends[chunk, angle : angle + 1] = carry
             rises, carry = [None] * groups, None
             for group in reversed(range(groups)):
                 item = rise[group]
@@ -484,11 +498,14 @@
                     item = item + local[7, :, where] * carry
                 carry = item[:1]
                 rises[group] = item
-            ends[first // LANES, angles + angle : angles + angle + 1] = carry
+            ends[chunk, angles + angle : angles + angle + 1] = carry
             for group in range(groups):
                 out[angle, group * GROUP : (group + 1) * GROUP, where] = gain * (
                     falls[group] + rises[group] - value[group]
                 )
+        return 0
+
+    lax.fori_loop(0, width // LANES, scan, 0)
 
 
 def inverse_kernel(
@@ -497,11 +514,12 @@
     angles, strip, width = value.shape
     half = width // 2
     groups = strip // GROUP
-    for first in range(0, width, LANES):
-        where = slice(first, first + LANES)
+
+    def enter(chunk, _):
+        where = pl.ds(pl.multiple_of(chunk * LANES, LANES), LANES)
         for angle in range(angles):
-            fall = incoming[first // LANES, angle : angle + 1]
-            rise = incoming[first // LANES, angles + angle : angles + angle + 1]
+            fall = incoming[chunk, angle : angle + 1]
+            rise = incoming[chunk, angles + angle : angles + angle + 1]
             step = extra[2:3, where]
             falls, rises = [], []
             for group in range(groups):
@@ -522,6 +540,9 @@
                 start = angle * strip + pair * GROUP
                 xh[start : start + 2 * GROUP, where] = rounded
                 xl[start : start + 2 * GROUP, where] = (item - rounded.astype(f32)).astype(bf16)
+        return 0
+
+    lax.fori_loop(0, width // LANES, enter, 0)
     last = (((1,), (1,)), ((), ()))
     for first in range(0, half, TILE):
         where = slice(first, first + TILE)
@@ -566,6 +587,7 @@
             pltpu.SemaphoreType.DMA(((reach + 1) * cap,)),
         ],
         compiler_params=params(),
+        cost_estimate=cost(2),
         name="cut",
     )(tables, object_field)
     arrived = exchanged(cuts, reach, [(j, j - 1, -j) for j in range(1, reach + 1)], [], 1, "fetch")
@@ -577,9 +599,7 @@
         in_specs=[vmem],
         out_specs=[vmem] * 4,
         compiler_params=params(),
-        cost_estimate=pl.CostEstimate(
-            flops=half * half * 10, bytes_accessed=half * half * 8, transcendentals=0
-        ),
+        cost_estimate=cost(2),
         name="tables",
     )(factors)
     local, powers, extra = decay_tables(width, strip)
@@ -599,16 +619,19 @@
         out_specs=[vmem, vmem],
         scratch_shapes=[pltpu.VMEM(((reach + 1) * strip, side), f32)],
         compiler_params=params(),
+        cost_estimate=cost(4),
         name="frames",
     )(frame_table, frame_count, probe, measured, cos_part, sin_part, cuts, arrived)
     landed = exchanged(away, reach, [(j - 1, j - 1, j) for j in range(1, reach + 1)], [], 2, "give")
 
-    updated, edges = pl.pallas_call(
+    updated, held, edges = pl.pallas_call(
         place_kernel,
-        out_shape=[shape(object_field.shape, f32), shape((2, angles, 2, 1, width), f32)],
+        out_shape=[shape(object_field.shape, f32)] * 2 + [shape((2, angles, 2, 1, width), f32)],
         in_specs=[smem, vmem, vmem, vmem],
-        out_specs=[vmem, vmem],
+        out_specs=[hbm, vmem, vmem],
+        scratch_shapes=[pltpu.SemaphoreType.DMA],
         compiler_params=params(),
+        cost_estimate=cost(3),
         name="place",
     )(tables, object_field, own, landed)
     halo = exchanged(edges, 2, [(1, 0, 1), (0, 1, -1)], [], 3, "edges")
@@ -620,8 +643,9 @@
         out_specs=[vmem, vmem],
         scratch_shapes=[pltpu.VMEM((rows, width), f32)] + [pltpu.VMEM((rows, half), bf16)] * 4,
         compiler_params=params(),
+        cost_estimate=cost(9),
         name="forward",
-    )(updated, halo, *half_tables, local, extra)
+    )(held, halo, *half_tables, local, extra)
     incoming = pl.pallas_call(
         join_kernel,
         out_shape=shape(ends.shape, f32),
@@ -636,6 +660,7 @@
             pltpu.SemaphoreType.DMA((blocks,)),
         ],
         compiler_params=params(collective_id=4, has_side_effects=True),
+        cost_estimate=cost(10),
         name="join",
     )(ends, by_block(powers), by_block(extra))
     phase_map = pl.pallas_call(
@@ -648,6 +673,7 @@
             pltpu.VMEM((rows, width), bf16),
         ],
         compiler_params=params(),
+        cost_estimate=cost(6),
         name="inverse",
     )(solved, incoming, *half_tables, local, extra)
     return (updated, phase_map)

time: 79.8 us -> 79.6 us (level)
  local copies, waits for them, and re-layouts: 5.09 us -> 2.91 us
  Pallas kernels: 73 us -> 75 us
    unnamed x26 -> x24, local copies, waits for them, and re-layouts: 5.09 us -> 2.91 us
    pallas_call x1, Pallas kernels: 9.35 us -> 11.3 us  [body(): pl.pallas_call(forward_kernel, out_shape=[shape((angles, strip, width), f...]
where the time goes in v3:
time: 79.6 us; the launch traced here: 79.4 us
  Pallas kernels  75 us (94%)
  local copies, waits for them, and re-layouts  2.91 us (4%)
  between operations  1.5 us (2%)
    pallas_call x4, Pallas kernels, exchanged(): pl.pallas_call(functools.partial(exchange_kernel, moves, keep), out_shape...  29.3 us
    pallas_call x1, Pallas kernels, body(): pl.pallas_call(join_kernel, out_shape=shape(ends.shape, f32), in_specs=[v...  16 us
    pallas_call x1, Pallas kernels, body(): pl.pallas_call(forward_kernel, out_shape=[shape((angles, strip, width), f...  11.3 us
    pallas_call x1, Pallas kernels, body(): pl.pallas_call(inverse_kernel, out_shape=shape((angles, strip, width), f3...  6.83 us
    pallas_call x1, Pallas kernels, body(): pl.pallas_call(frame_kernel, out_shape=[shape((cap, 2, strip, side), f32)...  4.3 us
    pallas_call x1, Pallas kernels, body(): pl.pallas_call(place_kernel, out_shape=[shape(object_field.shape, f32)] *...  3.38 us
    unnamed x24, local copies, waits for them, and re-layouts  2.91 us
    pallas_call x1, Pallas kernels, body(): pl.pallas_call(table_kernel, out_shape=[shape((half, half), bf16)] * 4, i...  2.05 us

profile of v3, /device:TPU:0, one launch (start us, length us, event | category | flops | bytes accessed | tf_op | source)
XLA Modules:
  0.0 79.4 jit_solution(16126961678169672965)
XLA Ops:
  1.3 0.0 copy-start.11
  1.3 0.7 copy-done.11
  2.0 4.3 %tell.1.tables = s32[3,2,3]{2,1,0:T(2,128)S(1)} custom-call(s32[1,2,3]{2,1,0:T(2,128)S(1)} %bitcast.1), custom_call_target="tpu_custom_call" | custom-call | bytes 12000000 | tf_op jit(solution)/shard_map/tell/pallas_call | solution.py:82
  6.3 0.0 copy-start
  6.3 2.2 %copy-done = f32[2,2,128,2048]{3,2,1,0:T(8,128)S(1)} copy-done((f32[2,2,128,2048]{3,2,1,0:T(8,128)S(1)}, f32[2,2,128,2048]{3,2,1,0:T(8,128)}, u32[]{:S(2)}) %copy-start) | copy-done | bytes 4194328
  8.5 1.9 %cut.1.source.cuts = bf16[3,2,2,128,256]{4,3,2,1,0:T(8,128)(2,1)S(1)} custom-call(s32[3,2,3]{2,1,0:T(2,128)S(1)} %tell.1.tables, f32[2,2,128,2048]{3,2,1,0:T(8,128)S(1)} %copy-done), custom_call_target="tpu_custom_call" | custom-call | bytes 6000000 | tf_op jit(solution)/shard_map/cut/pallas_call | solution.py:580
  10.4 0.0 copy-start.1
  10.4 14.2 %fetch.1.arrived = bf16[2,2,2,128,256]{4,3,2,1,0:T(8,128)(2,1)S(1)} custom-call(bf16[3,2,2,128,256]{4,3,2,1,0:T(8,128)(2,1)S(1)} %cut.1.source.cuts), custom_call_target="tpu_custom_call" | custom-call | bytes 12000000 | tf_op jit(solution)/shard_map/fetch/pallas_call | solution.py:82
  24.6 0.0 copy-done.4
  24.6 0.0 copy-done.6
  24.6 0.0 copy-done.8
  24.6 4.3 %frames.1 = (f32[2,2,128,256]{3,2,1,0:T(8,128)S(1)}, bf16[2,2,2,128,256]{4,3,2,1,0:T(8,128)(2,1)S(1)}) custom-call(s32[2,3]{1,0:T(2,128)S(1)} %copy-done.11, s32[1]{0:T(128)S(6)} %copy.14.counts, f32[2,256,256]{2,1,0:T(8,128)S(1)} %copy-done.4, bf16[2,256,256]{2,1,0:T(8,128)(2,1)S(1)} %copy-done.6, bf16[256,256]{1,0:T(8,128)(2,1)S(1)} %copy-done.9, ...), custom_call_target="tpu_custom_call" | custom-call | bytes 12000000 | tf_op jit(solution)/shard_map/frames/pallas_call | solution.py:612
  28.9 7.4 %give.1.away_ref = bf16[2,2,2,128,256]{4,3,2,1,0:T(8,128)(2,1)S(1)} custom-call(bf16[2,2,2,128,256]{4,3,2,1,0:T(8,128)(2,1)S(1)} %get-tuple-element.14.source), custom_call_target="tpu_custom_call" | custom-call | bytes 12000000 | tf_op jit(solution)/shard_map/give/pallas_call | solution.py:82
  36.3 0.0 copy-start.3
  36.3 0.0 copy-start.2
  36.4 0.0 copy-start.5
  36.4 3.4 %place.1 = (f32[2,2,128,2048]{3,2,1,0:T(8,128)}, f32[2,2,128,2048]{3,2,1,0:T(8,128)S(1)}, f32[2,2,2,1,2048]{4,3,2,1,0:T(1,128)S(1)}) custom-call(s32[3,2,3]{2,1,0:T(2,128)S(1)} %tell.1.tables, f32[2,2,128,2048]{3,2,1,0:T(8,128)S(1)} %copy-done.1, f32[2,2,128,256]{3,2,1,0:T(8,128)S(1)} %get-tuple-element.13.own, bf16[2,2,2,128,256]{4,3,2,1,0:T(8,128)(2,1)S(1)} %give.1.away_ref), custom_call_target="tpu_custom_call" | custom-call | bytes 9000000 | tf_op jit(solution)/shard_map/place/pallas_call | solution.py:627
  39.8 3.4 %edges.1.halo = f32[2,2,2,1,2048]{4,3,2,1,0:T(1,128)S(1)} custom-call(f32[2,2,2,1,2048]{4,3,2,1,0:T(1,128)S(1)} %get-tuple-element.17.source), custom_call_target="tpu_custom_call" | custom-call | bytes 12000000 | tf_op jit(solution)/shard_map/edges/pallas_call | solution.py:82
  43.1 2.1 %tables.1 = (bf16[1024,1024]{1,0:T(8,128)(2,1)S(1)}, bf16[1024,1024]{1,0:T(8,128)(2,1)S(1)}, bf16[1024,1024]{1,0:T(8,128)(2,1)S(1)}, bf16[1024,1024]{1,0:T(8,128)(2,1)S(1)}) custom-call(f32[2,4,32,1024]{3,2,1,0:T(8,128)S(1)} %copy-done.3), custom_call_target="tpu_custom_call" | custom-call | bytes 6000000 | tf_op jit(solution)/shard_map/tables/pallas_call | solution.py:596
  45.2 0.0 copy-start.7
  45.2 0.0 copy-start.10
  45.2 11.3 %forward.1 = (f32[2,128,2048]{2,1,0:T(8,128)S(1)}, f32[16,4,128]{2,1,0:T(4,128)S(1)}) custom-call(f32[2,2,128,2048]{3,2,1,0:T(8,128)S(1)} %get-tuple-element.16.field, f32[2,2,2,1,2048]{4,3,2,1,0:T(1,128)S(1)} %edges.1.halo, bf16[1024,1024]{1,0:T(8,128)(2,1)S(1)} %get-tuple-element.18.even_hi, bf16[1024,1024]{1,0:T(8,128)(2,1)S(1)} %get-tuple-element.19.even_lo, ...), custom_call_target="tpu_custom_call" | custom-call | bytes 27000000 | tf_op jit(solution)/shard_map/forward/pallas_call | solution.py:639
  56.6 16.0 %join.1.incoming = f32[16,4,128]{2,1,0:T(4,128)S(1)} custom-call(f32[16,4,128]{2,1,0:T(4,128)S(1)} %get-tuple-element.23.ends, f32[16,17,128]{2,1,0:T(8,128)S(1)} %copy-done.7, f32[16,8,128]{2,1,0:T(8,128)S(1)} %copy-done.10), custom_call_target="tpu_custom_call" | custom-call | bytes 30000000 | tf_op jit(solution)/shard_map/join/pallas_call | solution.py:649
  72.6 6.8 %inverse.1 = f32[2,128,2048]{2,1,0:T(8,128)} custom-call(f32[2,128,2048]{2,1,0:T(8,128)S(1)} %get-tuple-element.22.value, f32[16,4,128]{2,1,0:T(4,128)S(1)} %join.1.incoming, bf16[1024,1024]{1,0:T(8,128)(2,1)S(1)} %get-tuple-element.18.even_hi, bf16[1024,1024]{1,0:T(8,128)(2,1)S(1)} %get-tuple-element.19.even_lo, ...), custom_call_target="tpu_custom_call" | custom-call | bytes 18000000 | tf_op jit(solution)/shard_map/inverse/pallas_call | solution.py:666
  (11 shorter events, 0.0 us)
Async XLA Ops:
  1.3 0.7 copy-start.11
  6.3 2.2 %copy-start = (f32[2,2,128,2048]{3,2,1,0:T(8,128)S(1)}, f32[2,2,128,2048]{3,2,1,0:T(8,128)}, u32[]{:S(2)}) copy-start(f32[2,2,128,2048]{3,2,1,0:T(8,128)} %field.3) | copy-start | bytes 12582916
  8.5 16.1 %copy-start.4 = (f32[2,256,256]{2,1,0:T(8,128)S(1)}, f32[2,256,256]{2,1,0:T(8,128)}, u32[]{:S(2)}) copy-start(f32[2,256,256]{2,1,0:T(8,128)} %probe.1) | copy-start | bytes 1572868
  8.5 16.1 %copy-start.6 = (bf16[2,256,256]{2,1,0:T(8,128)(2,1)S(1)}, bf16[2,256,256]{2,1,0:T(8,128)(2,1)}, u32[]{:S(2)}) copy-start(bf16[2,256,256]{2,1,0:T(8,128)(2,1)} %measured.1) | copy-start | bytes 786436
  8.5 16.1 %copy-start.8 = (bf16[256,256]{1,0:T(8,128)(2,1)S(1)}, bf16[256,256]{1,0:T(8,128)(2,1)}, u32[]{:S(2)}) copy-start(bf16[256,256]{1,0:T(8,128)(2,1)} %constant.25.sin_ref) | copy-start | bytes 393220
  8.5 16.1 %copy-start.9 = (bf16[256,256]{1,0:T(8,128)(2,1)S(1)}, bf16[256,256]{1,0:T(8,128)(2,1)}, u32[]{:S(2)}) copy-start(bf16[256,256]{1,0:T(8,128)(2,1)} %constant.24.cos_ref) | copy-start | bytes 393220
  10.4 25.9 %copy-start.1 = (f32[2,2,128,2048]{3,2,1,0:T(8,128)S(1)}, f32[2,2,128,2048]{3,2,1,0:T(8,128)}, u32[]{:S(2)}) copy-start(f32[2,2,128,2048]{3,2,1,0:T(8,128)} %field.3) | copy-start | bytes 12582916
  36.3 6.8 %copy-start.3 = (f32[2,4,32,1024]{3,2,1,0:T(8,128)S(1)}, f32[2,4,32,1024]{3,2,1,0:T(8,128)}, u32[]{:S(2)}) copy-start(f32[2,4,32,1024]{3,2,1,0:T(8,128)} %constant.14.clone.factors) | copy-start | bytes 3145732
  36.3 8.8 %copy-start.2 = (f32[8,8,2048]{2,1,0:T(8,128)S(1)}, f32[8,8,2048]{2,1,0:T(8,128)}, u32[]{:S(2)}) copy-start(f32[8,8,2048]{2,1,0:T(8,128)} %constant.17.clone.local) | copy-start | bytes 1572868
  36.4 8.8 %copy-start.5 = (f32[8,2048]{1,0:T(8,128)S(1)}, f32[8,2048]{1,0:T(8,128)}, u32[]{:S(2)}) copy-start(f32[8,2048]{1,0:T(8,128)} %constant.18.clone.extra) | copy-start | bytes 196612
  45.2 11.3 %copy-start.7 = (f32[16,17,128]{2,1,0:T(8,128)S(1)}, f32[16,17,128]{2,1,0:T(8,128)}, u32[]{:S(2)}) copy-start(f32[16,17,128]{2,1,0:T(8,128)} %constant.19.clone.powers) | copy-start | bytes 417796
  45.2 11.3 %copy-start.10 = (f32[16,8,128]{2,1,0:T(8,128)S(1)}, f32[16,8,128]{2,1,0:T(8,128)}, u32[]{:S(2)}) copy-start(f32[16,8,128]{2,1,0:T(8,128)} %constant.20.clone.extra) | copy-start | bytes 196612

commit v4 on v2

--- a/solution.py
+++ b/solution.py
@@ -22,19 +22,28 @@
 MESH = pl.DeviceIdType.MESH
 vmem = pl.BlockSpec(memory_space=pltpu.VMEM)
 smem = pl.BlockSpec(memory_space=pltpu.SMEM)
-hbm = pl.BlockSpec(memory_space=pl.ANY)
+hbm = pl.BlockSpec(memory_space=pltpu.HBM)
+
+
+def cost(micros):
+    return pl.CostEstimate(
+        flops=0, bytes_accessed=int(micros * 3_000_000), transcendentals=0
+    )
 
 
 def params(**more):
     return pltpu.CompilerParams(vmem_limit_bytes=VMEM_BYTES, **more)
 
 
-def exchange_kernel(moves, keep, source, out, send_sems, recv_sems):
+def exchange_kernel(moves, keep, *refs):
+    arrays = (len(refs) - 2) // 2
+    sources, outs = refs[:arrays], refs[arrays : 2 * arrays]
+    send_sems, recv_sems = refs[2 * arrays :]
     count = lax.axis_size("tile")
     me = lax.axis_index("tile")
     barrier = pltpu.get_barrier_semaphore()
     met = jnp.zeros((), jnp.int32)
-    for by in sorted({sign * by for _, _, by in moves for sign in (1, -1)}):
+    for by in sorted({sign * by for *_, by in moves for sign in (1, -1)}):
         there = (me + by >= 0) & (me + by < count)
 
         @pl.when(there)
@@ -46,10 +55,10 @@
         met = met + jnp.where(there, 1, 0)
     pl.semaphore_wait(barrier, met)
     copies = []
-    for index, (first, last, by) in enumerate(moves):
+    for index, (array, first, last, by) in enumerate(moves):
         copy = pltpu.make_async_remote_copy(
-            src_ref=source.at[first],
-            dst_ref=out.at[last],
+            src_ref=sources[array].at[first],
+            dst_ref=outs[array].at[last],
             send_sem=send_sems.at[index],
             recv_sem=recv_sems.at[index],
             device_id={"tile": me + by},
@@ -57,31 +66,35 @@
         )
         sends = (me + by >= 0) & (me + by < count)
         takes = (me - by >= 0) & (me - by < count)
-        copies.append((copy, sends, takes, last))
+        copies.append((copy, sends, takes, outs[array], last))
         pl.when(sends)(copy.start)
-    for first, last in keep:
-        out[last] = source[first]
-    for copy, sends, takes, last in copies:
+    for array, first, last in keep:
+        outs[array][last] = sources[array][first]
+    for copy, sends, takes, out, last in copies:
 
         @pl.when(jnp.logical_not(takes))
         def _():
             out[last] = jnp.zeros(out.shape[1:], out.dtype)
 
-    for copy, sends, takes, last in copies:
+    for copy, sends, takes, out, last in copies:
         pl.when(takes)(copy.wait_recv)
         pl.when(sends)(copy.wait_send)
 
 
-def exchanged(source, slots, moves, keep, number, name):
+def exchanged(sources, slots, moves, keep, number, name):
     return pl.pallas_call(
         functools.partial(exchange_kernel, moves, keep),
-        out_shape=jax.ShapeDtypeStruct((slots,) + source.shape[1:], source.dtype),
-        in_specs=[vmem],
-        out_specs=vmem,
+        out_shape=[
+            jax.ShapeDtypeStruct((slot,) + source.shape[1:], source.dtype)
+            for slot, source in zip(slots, sources)
+        ],
+        in_specs=[vmem] * len(sources),
+        out_specs=[vmem] * len(sources),
         scratch_shapes=[pltpu.SemaphoreType.DMA((len(moves),))] * 2,
         compiler_params=params(collective_id=number, has_side_effects=True),
+        cost_estimate=cost(4),
         name=name,
-    )(source)
+    )(*sources)
 
 
 def join_kernel(ends, powers, extra, out, heard, told, up_sems, in_sems, down_sems, back_sems):
@@ -267,7 +280,7 @@
 
 
 def cut_kernel(tables, field, out, buffer, sems):
-    count, cap = tables.shape[0], tables.shape[1]
+    count, cap = out.shape[0], out.shape[1]
     width = field.shape[3]
     side = out.shape[-1]
     span = side + LANES
@@ -292,12 +305,14 @@
 
 
 def frame_kernel(
-    table, counts, probe, measured, cos_ref, sin_ref, cuts, arrived, own_out, away_out, window
+    tables, probe, moved, cos_ref, sin_ref, arrived, own_out, away_out, window
 ):
-    pieces = [cuts.at[0]] + [arrived.at[j] for j in range(arrived.shape[0])]
+    pieces = [arrived.at[j] for j in range(arrived.shape[0])]
+    measured = moved.at[0]
     cap, side = measured.shape[0], measured.shape[1]
     strip = pieces[0].shape[2]
     reach = len(pieces) - 1
+    middle = reach // 2
     total = (reach + 1) * strip
     cos_part, sin_part = cos_ref[...], sin_ref[...]
     stacked = jnp.concatenate([cos_part, sin_part], 0)
@@ -322,7 +337,7 @@
         return (rc - js, rs + ic) if sign > 0 else (rc + js, ic - rs)
 
     for s in range(cap):
-        offset = table[s, 0]
+        offset = tables[middle, s, 0]
         patch = []
         for part in range(2):
             for j in range(reach + 1):
@@ -339,7 +354,7 @@
             (spec_re * factor).astype(bf16), (spec_im * factor).astype(bf16), -1
         )
         corr_re, corr_im = right(back_re.astype(bf16), back_im.astype(bf16), -1)
-        live = s < counts[0]
+        live = s < tables[middle, cap, 0]
         updates = (
             (probe_re * corr_re + probe_im * corr_im) / peak,
             (probe_re * corr_im - probe_im * corr_re) / peak,
@@ -348,19 +363,23 @@
             window[...] = jnp.zeros_like(window)
             window[:side] = jnp.where(live, updates[part], 0.0)
             turned = pltpu.roll(window[...], offset, 0)
-            own_out[s, part] = turned[:strip]
-            for j in range(1, reach + 1):
-                away_out[j - 1, s, part] = turned[j * strip : (j + 1) * strip].astype(bf16)
-
-
-def place_kernel(tables, field, own, away_ref, out, edges):
-    away = [away_ref.at[j] for j in range(away_ref.shape[0])]
+            for j in range(reach + 1):
+                piece = turned[j * strip : (j + 1) * strip]
+                if j == middle:
+                    own_out[s, part] = piece
+                else:
+                    away_out[j, s, part] = piece.astype(bf16)
+
+
+def place_kernel(tables, field, own, away_ref, updated, out, edges, sem):
+    pieces = [away_ref.at[j] for j in range(away_ref.shape[0])]
+    pieces[(len(pieces) - 1) // 2] = own
     width = field.shape[3]
     cap, side = own.shape[0], own.shape[3]
     span = side + LANES
     out[...] = field[...]
     pad = jnp.zeros((own.shape[2], LANES), f32)
-    for j, source in enumerate((own, *away)):
+    for j, source in enumerate(pieces):
         for s in range(cap):
             column = tables[j, s, 1]
             start = pl.multiple_of(window_start(column, width, span), LANES)
@@ -377,6 +396,9 @@
         for part in range(2):
             edges[0, angle, part] = out[angle, part, :1]
             edges[1, angle, part] = out[angle, part, strip - 1 :]
+    copy = pltpu.make_async_copy(out, updated, sem)
+    copy.start()
+    copy.wait()
 
 
 def mirror(value):
@@ -459,8 +481,9 @@
                 + jnp.dot(high[...], table_lo[:, where], preferred_element_type=f32)
             )
     groups = strip // GROUP
-    for first in range(0, width, LANES):
-        where = slice(first, first + LANES)
+
+    def scan(chunk, _):
+        where = pl.ds(pl.multiple_of(chunk * LANES, LANES), LANES)
         gain = extra[0:1, where]
         for angle in range(angles):
             value = source[angle * strip : (angle + 1) * strip, where]
@@ -476,7 +499,7 @@
                     item = item + local[3, :, where] * carry
                 carry = item[GROUP - 1 :]
                 falls.append(item)
-            ends[first // LANES, angle : angle + 1] = carry
+            ends[chunk, angle : angle + 1] = carry
             rises, carry = [None] * groups, None
             for group in reversed(range(groups)):
                 item = rise[group]
@@ -484,11 +507,14 @@
                     item = item + local[7, :, where] * carry
                 carry = item[:1]
                 rises[group] = item
-            ends[first // LANES, angles + angle : angles + angle + 1] = carry
+            ends[chunk, angles + angle : angles + angle + 1] = carry
             for group in range(groups):
                 out[angle, group * GROUP : (group + 1) * GROUP, where] = gain * (
                     falls[group] + rises[group] - value[group]
                 )
+        return 0
+
+    lax.fori_loop(0, width // LANES, scan, 0)
 
 
 def inverse_kernel(
@@ -497,11 +523,12 @@
     angles, strip, width = value.shape
     half = width // 2
     groups = strip // GROUP
-    for first in range(0, width, LANES):
-        where = slice(first, first + LANES)
+
+    def enter(chunk, _):
+        where = pl.ds(pl.multiple_of(chunk * LANES, LANES), LANES)
         for angle in range(angles):
-            fall = incoming[first // LANES, angle : angle + 1]
-            rise = incoming[first // LANES, angles + angle : angles + angle + 1]
+            fall = incoming[chunk, angle : angle + 1]
+            rise = incoming[chunk, angles + angle : angles + angle + 1]
             step = extra[2:3, where]
             falls, rises = [], []
             for group in range(groups):
@@ -522,6 +549,9 @@
                 start = angle * strip + pair * GROUP
                 xh[start : start + 2 * GROUP, where] = rounded
                 xl[start : start + 2 * GROUP, where] = (item - rounded.astype(f32)).astype(bf16)
+        return 0
+
+    lax.fori_loop(0, width // LANES, enter, 0)
     last = (((1,), (1,)), ((), ()))
     for first in range(0, half, TILE):
         where = slice(first, first + TILE)
@@ -553,8 +583,19 @@
     blocks = width // LANES
     shape = jax.ShapeDtypeStruct
 
-    tables = exchanged(
-        frame_table[None], reach + 1, [(0, j, j) for j in range(1, reach + 1)], [(0, 0)], 0, "tell"
+    middle = reach // 2
+    others = [j for j in range(reach + 1) if j != middle]
+    record = jnp.concatenate(
+        [frame_table, jnp.pad(frame_count[:, None], ((0, 0), (0, 2)))]
+    )
+    moves = [(0, 0, j, j) for j in range(1, reach + 1)]
+    keep = [(0, 0, 0)]
+    if middle:
+        moves.append((1, 0, 0, middle))
+    else:
+        keep.append((1, 0, 0))
+    tables, moved = exchanged(
+        [record[None], measured[None]], [reach + 1, 1], moves, keep, 0, "tell"
     )
     cuts = pl.pallas_call(
         cut_kernel,
@@ -566,9 +607,12 @@
             pltpu.SemaphoreType.DMA(((reach + 1) * cap,)),
         ],
         compiler_params=params(),
+        cost_estimate=cost(2),
         name="cut",
     )(tables, object_field)
-    arrived = exchanged(cuts, reach, [(j, j - 1, -j) for j in range(1, reach + 1)], [], 1, "fetch")
+    (arrived,) = exchanged(
+        [cuts], [reach + 1], [(0, j, j, middle - j) for j in others], [(0, middle, middle)], 1, "fetch"
+    )
 
     factors = cosine_factors(width)
     half_tables = pl.pallas_call(
@@ -577,9 +621,7 @@
         in_specs=[vmem],
         out_specs=[vmem] * 4,
         compiler_params=params(),
-        cost_estimate=pl.CostEstimate(
-            flops=half * half * 10, bytes_accessed=half * half * 8, transcendentals=0
-        ),
+        cost_estimate=cost(2),
         name="tables",
     )(factors)
     local, powers, extra = decay_tables(width, strip)
@@ -593,25 +635,30 @@
         frame_kernel,
         out_shape=[
             shape((cap, 2, strip, side), f32),
-            shape((reach, cap, 2, strip, side), bf16),
+            shape((reach + 1, cap, 2, strip, side), bf16),
         ],
-        in_specs=[smem, smem] + [vmem] * 6,
+        in_specs=[smem] + [vmem] * 5,
         out_specs=[vmem, vmem],
         scratch_shapes=[pltpu.VMEM(((reach + 1) * strip, side), f32)],
         compiler_params=params(),
+        cost_estimate=cost(4),
         name="frames",
-    )(frame_table, frame_count, probe, measured, cos_part, sin_part, cuts, arrived)
-    landed = exchanged(away, reach, [(j - 1, j - 1, j) for j in range(1, reach + 1)], [], 2, "give")
-
-    updated, edges = pl.pallas_call(
+    )(tables, probe, moved, cos_part, sin_part, arrived)
+    (landed,) = exchanged(
+        [away], [reach + 1], [(0, j, j, j - middle) for j in others], [], 2, "give"
+    )
+
+    updated, held, edges = pl.pallas_call(
         place_kernel,
-        out_shape=[shape(object_field.shape, f32), shape((2, angles, 2, 1, width), f32)],
+        out_shape=[shape(object_field.shape, f32)] * 2 + [shape((2, angles, 2, 1, width), f32)],
         in_specs=[smem, vmem, vmem, vmem],
-        out_specs=[vmem, vmem],
+        out_specs=[hbm, vmem, vmem],
+        scratch_shapes=[pltpu.SemaphoreType.DMA],
         compiler_params=params(),
+        cost_estimate=cost(3),
         name="place",
     )(tables, object_field, own, landed)
-    halo = exchanged(edges, 2, [(1, 0, 1), (0, 1, -1)], [], 3, "edges")
+    (halo,) = exchanged([edges], [2], [(0, 1, 0, 1), (0, 0, 1, -1)], [], 3, "edges")
 
     solved, ends = pl.pallas_call(
         forward_kernel,
@@ -620,8 +667,9 @@
         out_specs=[vmem, vmem],
         scratch_shapes=[pltpu.VMEM((rows, width), f32)] + [pltpu.VMEM((rows, half), bf16)] * 4,
         compiler_params=params(),
+        cost_estimate=cost(9),
         name="forward",
-    )(updated, halo, *half_tables, local, extra)
+    )(held, halo, *half_tables, local, extra)
     incoming = pl.pallas_call(
         join_kernel,
         out_shape=shape(ends.shape, f32),
@@ -636,6 +684,7 @@
             pltpu.SemaphoreType.DMA((blocks,)),
         ],
         compiler_params=params(collective_id=4, has_side_effects=True),
+        cost_estimate=cost(10),
         name="join",
     )(ends, by_block(powers), by_block(extra))
     phase_map = pl.pallas_call(
@@ -648,6 +697,7 @@
             pltpu.VMEM((rows, width), bf16),
         ],
         compiler_params=params(),
+        cost_estimate=cost(6),
         name="inverse",
     )(solved, incoming, *half_tables, local, extra)
     return (updated, phase_map)

time: 79.8 us -> 75 us (0.940)
  Pallas kernels: 73 us -> 69.5 us
  local copies, waits for them, and re-layouts: 5.09 us -> 3.18 us
    pallas_call x1, Pallas kernels: 16.2 us -> 13.7 us  [body(): pl.pallas_call(join_kernel, out_shape=shape(ends.shape, f32), in_specs=[v...]
    pallas_call x4, Pallas kernels: 29.2 us -> 27.1 us  [exchanged(): pl.pallas_call(functools.partial(exchange_kernel, moves, keep), out_shape...]
    unnamed x26 -> x22, local copies, waits for them, and re-layouts: 5.09 us -> 3.18 us
where the time goes in v4:
time: 75 us; the launch traced here: 74.8 us
  Pallas kernels  69.5 us (93%)
  local copies, waits for them, and re-layouts  3.18 us (4%)
  between operations  1.47 us (2%)
    pallas_call x4, Pallas kernels, exchanged(): pl.pallas_call(functools.partial(exchange_kernel, moves, keep), out_shape...  27.1 us
    pallas_call x1, Pallas kernels, body(): pl.pallas_call(join_kernel, out_shape=shape(ends.shape, f32), in_specs=[v...  13.7 us
    pallas_call x1, Pallas kernels, body(): pl.pallas_call(forward_kernel, out_shape=[shape((angles, strip, width), f...  10 us
    pallas_call x1, Pallas kernels, body(): pl.pallas_call(inverse_kernel, out_shape=shape((angles, strip, width), f3...  6.83 us
    pallas_call x1, Pallas kernels, body(): pl.pallas_call(frame_kernel, out_shape=[shape((cap, 2, strip, side), f32)...  4.4 us
    pallas_call x1, Pallas kernels, body(): pl.pallas_call(place_kernel, out_shape=[shape(object_field.shape, f32)] *...  3.43 us
    unnamed x22, local copies, waits for them, and re-layouts  3.18 us
    pallas_call x1, Pallas kernels, body(): pl.pallas_call(table_kernel, out_shape=[shape((half, half), bf16)] * 4, i...  2.05 us

profile of v4, /device:TPU:0, one launch (start us, length us, event | category | flops | bytes accessed | tf_op | source)
XLA Modules:
  0.0 74.8 jit_solution(3823658018583913845)
XLA Ops:
  1.3 0.7 fusion.refs_0_
  2.0 0.9 %copy-done.6 = bf16[2,256,256]{2,1,0:T(8,128)(2,1)S(1)} copy-done((bf16[2,256,256]{2,1,0:T(8,128)(2,1)S(1)}, bf16[2,256,256]{2,1,0:T(8,128)(2,1)}, u32[]{:S(2)}) %copy-start.6) | copy-done | bytes 262168
  2.9 4.4 %tell.1 = (s32[3,3,3]{2,1,0:T(4,128)S(1)}, bf16[1,2,256,256]{3,2,1,0:T(8,128)(2,1)S(1)}) custom-call(s32[1,3,3]{2,1,0:T(4,128)S(1)} %fusion.refs_0_, bf16[1,2,256,256]{3,2,1,0:T(8,128)(2,1)S(1)} %bitcast.5), custom_call_target="tpu_custom_call" | custom-call | bytes 12000000 | tf_op jit(solution)/shard_map/tell/pallas_call | solution.py:85
  7.3 0.0 copy-start
  7.3 2.2 %copy-done = f32[2,2,128,2048]{3,2,1,0:T(8,128)S(1)} copy-done((f32[2,2,128,2048]{3,2,1,0:T(8,128)S(1)}, f32[2,2,128,2048]{3,2,1,0:T(8,128)}, u32[]{:S(2)}) %copy-start) | copy-done | bytes 4194328
  9.5 1.9 %cut.1.refs_0_ = bf16[3,2,2,128,256]{4,3,2,1,0:T(8,128)(2,1)S(1)} custom-call(s32[3,3,3]{2,1,0:T(4,128)S(1)} %get-tuple-element.15.tables, f32[2,2,128,2048]{3,2,1,0:T(8,128)S(1)} %copy-done), custom_call_target="tpu_custom_call" | custom-call | bytes 6000000 | tf_op jit(solution)/shard_map/cut/pallas_call | solution.py:600
  11.4 0.0 copy-start.1
  11.4 5.8 %fetch.1.arrived = bf16[3,2,2,128,256]{4,3,2,1,0:T(8,128)(2,1)S(1)} custom-call(bf16[3,2,2,128,256]{4,3,2,1,0:T(8,128)(2,1)S(1)} %cut.1.refs_0_), custom_call_target="tpu_custom_call" | custom-call | bytes 12000000 | tf_op jit(solution)/shard_map/fetch/pallas_call | solution.py:85
  17.2 0.0 copy-done.4
  17.2 0.0 copy-done.8
  17.2 4.4 %frames.1 = (f32[2,2,128,256]{3,2,1,0:T(8,128)S(1)}, bf16[3,2,2,128,256]{4,3,2,1,0:T(8,128)(2,1)S(1)}) custom-call(s32[3,3,3]{2,1,0:T(4,128)S(1)} %get-tuple-element.15.tables, f32[2,256,256]{2,1,0:T(8,128)S(1)} %copy-done.4, bf16[1,2,256,256]{3,2,1,0:T(8,128)(2,1)S(1)} %get-tuple-element.16.moved, bf16[256,256]{1,0:T(8,128)(2,1)S(1)} %copy-done.9, ...), custom_call_target="tpu_custom_call" | custom-call | bytes 12000000 | tf_op jit(solution)/shard_map/frames/pallas_call | solution.py:634
  21.6 8.7 %give.1.away_ref = bf16[3,2,2,128,256]{4,3,2,1,0:T(8,128)(2,1)S(1)} custom-call(bf16[3,2,2,128,256]{4,3,2,1,0:T(8,128)(2,1)S(1)} %get-tuple-element.18.refs_0_), custom_call_target="tpu_custom_call" | custom-call | bytes 12000000 | tf_op jit(solution)/shard_map/give/pallas_call | solution.py:85
  30.3 0.0 copy-start.3
  30.3 0.0 copy-start.2
  30.4 0.0 copy-start.5
  30.4 3.4 %place.1 = (f32[2,2,128,2048]{3,2,1,0:T(8,128)}, f32[2,2,128,2048]{3,2,1,0:T(8,128)S(1)}, f32[2,2,2,1,2048]{4,3,2,1,0:T(1,128)S(1)}) custom-call(s32[3,3,3]{2,1,0:T(4,128)S(1)} %get-tuple-element.15.tables, f32[2,2,128,2048]{3,2,1,0:T(8,128)S(1)} %copy-done.1, f32[2,2,128,256]{3,2,1,0:T(8,128)S(1)} %get-tuple-element.17.own, ...), custom_call_target="tpu_custom_call" | custom-call | bytes 9000000 | tf_op jit(solution)/shard_map/place/pallas_call | solution.py:651
  33.8 8.3 %edges.1.halo = f32[2,2,2,1,2048]{4,3,2,1,0:T(1,128)S(1)} custom-call(f32[2,2,2,1,2048]{4,3,2,1,0:T(1,128)S(1)} %get-tuple-element.21.refs_0_), custom_call_target="tpu_custom_call" | custom-call | bytes 12000000 | tf_op jit(solution)/shard_map/edges/pallas_call | solution.py:85
  42.1 0.0 copy-done.3
  42.2 2.1 %tables.1 = (bf16[1024,1024]{1,0:T(8,128)(2,1)S(1)}, bf16[1024,1024]{1,0:T(8,128)(2,1)S(1)}, bf16[1024,1024]{1,0:T(8,128)(2,1)S(1)}, bf16[1024,1024]{1,0:T(8,128)(2,1)S(1)}) custom-call(f32[2,4,32,1024]{3,2,1,0:T(8,128)S(1)} %copy-done.3), custom_call_target="tpu_custom_call" | custom-call | bytes 6000000 | tf_op jit(solution)/shard_map/tables/pallas_call | solution.py:618
  44.2 0.0 copy-start.7
  44.2 0.0 copy-start.10
  44.3 10.0 %forward.1 = (f32[2,128,2048]{2,1,0:T(8,128)S(1)}, f32[16,4,128]{2,1,0:T(4,128)S(1)}) custom-call(f32[2,2,128,2048]{3,2,1,0:T(8,128)S(1)} %get-tuple-element.20.field, f32[2,2,2,1,2048]{4,3,2,1,0:T(1,128)S(1)} %edges.1.halo, bf16[1024,1024]{1,0:T(8,128)(2,1)S(1)} %get-tuple-element.22.even_hi, bf16[1024,1024]{1,0:T(8,128)(2,1)S(1)} %get-tuple-element.23.even_lo, ...), custom_call_target="tpu_custom_call" | custom-call | bytes 27000000 | tf_op jit(solution)/shard_map/forward/pallas_call | solution.py:663
  54.3 13.7 %join.1.incoming = f32[16,4,128]{2,1,0:T(4,128)S(1)} custom-call(f32[16,4,128]{2,1,0:T(4,128)S(1)} %get-tuple-element.27.ends, f32[16,17,128]{2,1,0:T(8,128)S(1)} %copy-done.7, f32[16,8,128]{2,1,0:T(8,128)S(1)} %copy-done.10), custom_call_target="tpu_custom_call" | custom-call | bytes 30000000 | tf_op jit(solution)/shard_map/join/pallas_call | solution.py:673
  68.0 6.8 %inverse.1 = f32[2,128,2048]{2,1,0:T(8,128)} custom-call(f32[2,128,2048]{2,1,0:T(8,128)S(1)} %get-tuple-element.26.value, f32[16,4,128]{2,1,0:T(4,128)S(1)} %join.1.incoming, bf16[1024,1024]{1,0:T(8,128)(2,1)S(1)} %get-tuple-element.22.even_hi, bf16[1024,1024]{1,0:T(8,128)(2,1)S(1)} %get-tuple-element.23.even_lo, ...), custom_call_target="tpu_custom_call" | custom-call | bytes 18000000 | tf_op jit(solution)/shard_map/inverse/pallas_call | solution.py:690
  (10 shorter events, 0.0 us)
Async XLA Ops:
  2.0 0.9 %copy-start.6 = (bf16[2,256,256]{2,1,0:T(8,128)(2,1)S(1)}, bf16[2,256,256]{2,1,0:T(8,128)(2,1)}, u32[]{:S(2)}) copy-start(bf16[2,256,256]{2,1,0:T(8,128)(2,1)} %param.14) | copy-start | bytes 786436
  7.3 2.2 %copy-start = (f32[2,2,128,2048]{3,2,1,0:T(8,128)S(1)}, f32[2,2,128,2048]{3,2,1,0:T(8,128)}, u32[]{:S(2)}) copy-start(f32[2,2,128,2048]{3,2,1,0:T(8,128)} %field.3) | copy-start | bytes 12582916
  9.5 7.7 %copy-start.4 = (f32[2,256,256]{2,1,0:T(8,128)S(1)}, f32[2,256,256]{2,1,0:T(8,128)}, u32[]{:S(2)}) copy-start(f32[2,256,256]{2,1,0:T(8,128)} %probe.1) | copy-start | bytes 1572868
  9.5 7.7 %copy-start.8 = (bf16[256,256]{1,0:T(8,128)(2,1)S(1)}, bf16[256,256]{1,0:T(8,128)(2,1)}, u32[]{:S(2)}) copy-start(bf16[256,256]{1,0:T(8,128)(2,1)} %constant.29.sin_ref) | copy-start | bytes 393220
  9.5 7.7 %copy-start.9 = (bf16[256,256]{1,0:T(8,128)(2,1)S(1)}, bf16[256,256]{1,0:T(8,128)(2,1)}, u32[]{:S(2)}) copy-start(bf16[256,256]{1,0:T(8,128)(2,1)} %constant.28.cos_ref) | copy-start | bytes 393220
  11.4 18.9 %copy-start.1 = (f32[2,2,128,2048]{3,2,1,0:T(8,128)S(1)}, f32[2,2,128,2048]{3,2,1,0:T(8,128)}, u32[]{:S(2)}) copy-start(f32[2,2,128,2048]{3,2,1,0:T(8,128)} %field.3) | copy-start | bytes 12582916
  30.3 11.8 %copy-start.3 = (f32[2,4,32,1024]{3,2,1,0:T(8,128)S(1)}, f32[2,4,32,1024]{3,2,1,0:T(8,128)}, u32[]{:S(2)}) copy-start(f32[2,4,32,1024]{3,2,1,0:T(8,128)} %constant.16.clone.factors) | copy-start | bytes 3145732
  30.3 13.9 %copy-start.2 = (f32[8,8,2048]{2,1,0:T(8,128)S(1)}, f32[8,8,2048]{2,1,0:T(8,128)}, u32[]{:S(2)}) copy-start(f32[8,8,2048]{2,1,0:T(8,128)} %constant.19.clone.local) | copy-start | bytes 1572868
  30.4 13.9 %copy-start.5 = (f32[8,2048]{1,0:T(8,128)S(1)}, f32[8,2048]{1,0:T(8,128)}, u32[]{:S(2)}) copy-start(f32[8,2048]{1,0:T(8,128)} %constant.20.clone.extra) | copy-start | bytes 196612
  44.2 10.1 %copy-start.7 = (f32[16,17,128]{2,1,0:T(8,128)S(1)}, f32[16,17,128]{2,1,0:T(8,128)}, u32[]{:S(2)}) copy-start(f32[16,17,128]{2,1,0:T(8,128)} %constant.21.clone.powers) | copy-start | bytes 417796
  44.2 10.1 %copy-start.10 = (f32[16,8,128]{2,1,0:T(8,128)S(1)}, f32[16,8,128]{2,1,0:T(8,128)}, u32[]{:S(2)}) copy-start(f32[16,8,128]{2,1,0:T(8,128)} %constant.22.clone.extra) | copy-start | bytes 196612

commit v5 on v4

--- a/solution.py
+++ b/solution.py
@@ -35,10 +35,11 @@
     return pltpu.CompilerParams(vmem_limit_bytes=VMEM_BYTES, **more)
 
 
-def exchange_kernel(moves, keep, *refs):
-    arrays = (len(refs) - 2) // 2
-    sources, outs = refs[:arrays], refs[arrays : 2 * arrays]
-    send_sems, recv_sems = refs[2 * arrays :]
+def exchange_kernel(moves, keep, work, arrays, inputs, *refs):
+    sources, given = refs[:arrays], refs[arrays : arrays + inputs]
+    outs = refs[arrays + inputs : 2 * arrays + inputs]
+    made = refs[2 * arrays + inputs : -2]
+    send_sems, recv_sems = refs[-2:]
     count = lax.axis_size("tile")
     me = lax.axis_index("tile")
     barrier = pltpu.get_barrier_semaphore()
@@ -68,6 +69,8 @@
         takes = (me - by >= 0) & (me - by < count)
         copies.append((copy, sends, takes, outs[array], last))
         pl.when(sends)(copy.start)
+    if work is not None:
+        work(*given, *made)
     for array, first, last in keep:
         outs[array][last] = sources[array][first]
     for copy, sends, takes, out, last in copies:
@@ -81,20 +84,21 @@
         pl.when(sends)(copy.wait_send)
 
 
-def exchanged(sources, slots, moves, keep, number, name):
+def exchanged(sources, slots, moves, keep, number, name, work=None, given=(), made=()):
     return pl.pallas_call(
-        functools.partial(exchange_kernel, moves, keep),
+        functools.partial(exchange_kernel, moves, keep, work, len(sources), len(given)),
         out_shape=[
             jax.ShapeDtypeStruct((slot,) + source.shape[1:], source.dtype)
             for slot, source in zip(slots, sources)
-        ],
-        in_specs=[vmem] * len(sources),
-        out_specs=[vmem] * len(sources),
+        ]
+        + list(made),
+        in_specs=[vmem] * (len(sources) + len(given)),
+        out_specs=[vmem] * (len(sources) + len(made)),
         scratch_shapes=[pltpu.SemaphoreType.DMA((len(moves),))] * 2,
         compiler_params=params(collective_id=number, has_side_effects=True),
         cost_estimate=cost(4),
         name=name,
-    )(*sources)
+    )(*sources, *given)
 
 
 def join_kernel(ends, powers, extra, out, heard, told, up_sems, in_sems, down_sems, back_sems):
@@ -606,7 +610,7 @@
             pltpu.VMEM(((reach + 1) * cap, 2, strip, side + LANES), f32),
             pltpu.SemaphoreType.DMA(((reach + 1) * cap,)),
         ],
-        compiler_params=params(),
+        compiler_params=pltpu.CompilerParams(vmem_limit_bytes=2 * VMEM_BYTES),
         cost_estimate=cost(2),
         name="cut",
     )(tables, object_field)
@@ -615,15 +619,6 @@
     )
 
     factors = cosine_factors(width)
-    half_tables = pl.pallas_call(
-        table_kernel,
-        out_shape=[shape((half, half), bf16)] * 4,
-        in_specs=[vmem],
-        out_specs=[vmem] * 4,
-        compiler_params=params(),
-        cost_estimate=cost(2),
-        name="tables",
-    )(factors)
     local, powers, extra = decay_tables(width, strip)
 
     def by_block(table):
@@ -658,7 +653,10 @@
         cost_estimate=cost(3),
         name="place",
     )(tables, object_field, own, landed)
-    (halo,) = exchanged([edges], [2], [(0, 1, 0, 1), (0, 0, 1, -1)], [], 3, "edges")
+    halo, *half_tables = exchanged(
+        [edges], [2], [(0, 1, 0, 1), (0, 0, 1, -1)], [], 3, "edges",
+        table_kernel, [factors], [shape((half, half), bf16)] * 4,
+    )
 
     solved, ends = pl.pallas_call(
         forward_kernel,

time: 75 us -> 74.1 us (0.988)
    pallas_call x5 -> x4, Pallas kernels: 29.2 us -> 26.7 us  [exchanged(): pl.pallas_call(functools.partial(exchange_kernel, moves, keep, work, len(...]
    pallas_call x1, Pallas kernels: 1.93 us -> 4.17 us  [body(): pl.pallas_call(cut_kernel, out_shape=shape((reach + 1, cap, 2, strip, sid...]
    unnamed x22 -> x26, local copies, waits for them, and re-layouts: 3.18 us -> 2.72 us
where the time goes in v5:
time: 74.1 us; the launch traced here: 73.8 us
  Pallas kernels  68.9 us (93%)
  local copies, waits for them, and re-layouts  2.72 us (4%)
  between operations  1.49 us (2%)
    pallas_call x4, Pallas kernels, exchanged(): pl.pallas_call(functools.partial(exchange_kernel, moves, keep, work, len(...  26.7 us
    pallas_call x1, Pallas kernels, body(): pl.pallas_call(join_kernel, out_shape=shape(ends.shape, f32), in_specs=[v...  13.7 us
    pallas_call x1, Pallas kernels, body(): pl.pallas_call(forward_kernel, out_shape=[shape((angles, strip, width), f...  9.82 us
    pallas_call x1, Pallas kernels, body(): pl.pallas_call(inverse_kernel, out_shape=shape((angles, strip, width), f3...  6.83 us
    pallas_call x1, Pallas kernels, body(): pl.pallas_call(frame_kernel, out_shape=[shape((cap, 2, strip, side), f32)...  4.27 us
    pallas_call x1, Pallas kernels, body(): pl.pallas_call(cut_kernel, out_shape=shape((reach + 1, cap, 2, strip, sid...  4.17 us
    pallas_call x1, Pallas kernels, body(): pl.pallas_call(place_kernel, out_shape=[shape(object_field.shape, f32)] *...  3.41 us
    unnamed x26, local copies, waits for them, and re-layouts  2.72 us

profile of v5, /device:TPU:0, one launch (start us, length us, event | category | flops | bytes accessed | tf_op | source)
XLA Modules:
  0.0 73.8 jit_solution(7959951034225477662)
XLA Ops:
  1.3 0.7 fusion.refs_0_
  2.0 0.9 %copy-done.6 = bf16[2,256,256]{2,1,0:T(8,128)(2,1)S(1)} copy-done((bf16[2,256,256]{2,1,0:T(8,128)(2,1)S(1)}, bf16[2,256,256]{2,1,0:T(8,128)(2,1)}, u32[]{:S(2)}) %copy-start.6) | copy-done | bytes 262168
  2.9 4.4 %tell.1 = (s32[3,3,3]{2,1,0:T(4,128)S(1)}, bf16[1,2,256,256]{3,2,1,0:T(8,128)(2,1)S(1)}) custom-call(s32[1,3,3]{2,1,0:T(4,128)S(1)} %fusion.refs_0_, bf16[1,2,256,256]{3,2,1,0:T(8,128)(2,1)S(1)} %bitcast.5), custom_call_target="tpu_custom_call" | custom-call | bytes 12000000 | tf_op jit(solution)/shard_map/tell/pallas_call | solution.py:88
  7.3 0.0 copy-start.11
  7.3 0.6 copy-done.11
  7.9 4.2 %cut.1.refs_0_ = bf16[3,2,2,128,256]{4,3,2,1,0:T(8,128)(2,1)} custom-call(s32[3,3,3]{2,1,0:T(4,128)} %copy-done.11, f32[2,2,128,2048]{3,2,1,0:T(8,128)} %field.3), custom_call_target="tpu_custom_call" | custom-call | bytes 6000000 | tf_op jit(solution)/shard_map/cut/pallas_call | solution.py:604
  12.1 0.0 copy-start.1
  12.1 1.1 %copy-done.1 = bf16[3,2,2,128,256]{4,3,2,1,0:T(8,128)(2,1)S(1)} copy-done((bf16[3,2,2,128,256]{4,3,2,1,0:T(8,128)(2,1)S(1)}, bf16[3,2,2,128,256]{4,3,2,1,0:T(8,128)(2,1)}, u32[]{:S(2)}) %copy-start.1) | copy-done | bytes 786456
  13.2 5.3 %fetch.1.arrived = bf16[3,2,2,128,256]{4,3,2,1,0:T(8,128)(2,1)S(1)} custom-call(bf16[3,2,2,128,256]{4,3,2,1,0:T(8,128)(2,1)S(1)} %copy-done.1), custom_call_target="tpu_custom_call" | custom-call | bytes 12000000 | tf_op jit(solution)/shard_map/fetch/pallas_call | solution.py:88
  18.5 0.0 copy-done.4
  18.6 4.3 %frames.1 = (f32[2,2,128,256]{3,2,1,0:T(8,128)S(1)}, bf16[3,2,2,128,256]{4,3,2,1,0:T(8,128)(2,1)S(1)}) custom-call(s32[3,3,3]{2,1,0:T(4,128)S(1)} %copy-done.12, f32[2,256,256]{2,1,0:T(8,128)S(1)} %copy-done.4, bf16[1,2,256,256]{3,2,1,0:T(8,128)(2,1)S(1)} %get-tuple-element.17.moved, bf16[256,256]{1,0:T(8,128)(2,1)S(1)} %copy-done.9, ...), custom_call_target="tpu_custom_call" | custom-call | bytes 12000000 | tf_op jit(solution)/shard_map/frames/pallas_call | solution.py:629
  22.8 8.7 %give.1.away_ref = bf16[3,2,2,128,256]{4,3,2,1,0:T(8,128)(2,1)S(1)} custom-call(bf16[3,2,2,128,256]{4,3,2,1,0:T(8,128)(2,1)S(1)} %get-tuple-element.19.refs_0_), custom_call_target="tpu_custom_call" | custom-call | bytes 12000000 | tf_op jit(solution)/shard_map/give/pallas_call | solution.py:88
  31.5 0.0 copy-start.3
  31.6 0.0 copy-start.2
  31.6 0.0 copy-start.5
  31.6 3.4 %place.1 = (f32[2,2,128,2048]{3,2,1,0:T(8,128)}, f32[2,2,128,2048]{3,2,1,0:T(8,128)S(1)}, f32[2,2,2,1,2048]{4,3,2,1,0:T(1,128)S(1)}) custom-call(s32[3,3,3]{2,1,0:T(4,128)S(1)} %copy-done.12, f32[2,2,128,2048]{3,2,1,0:T(8,128)S(1)} %copy-done, f32[2,2,128,256]{3,2,1,0:T(8,128)S(1)} %get-tuple-element.18.own, bf16[3,2,2,128,256]{4,3,2,1,0:T(8,128)(2,1)S(1)} %give.1.away_ref), custom_call_target="tpu_custom_call" | custom-call | bytes 9000000 | tf_op jit(solution)/shard_map/place/pallas_call | solution.py:646
  35.0 8.3 %edges.1 = (f32[2,2,2,1,2048]{4,3,2,1,0:T(1,128)S(1)}, bf16[1024,1024]{1,0:T(8,128)(2,1)S(1)}, bf16[1024,1024]{1,0:T(8,128)(2,1)S(1)}, bf16[1024,1024]{1,0:T(8,128)(2,1)S(1)}, bf16[1024,1024]{1,0:T(8,128)(2,1)S(1)}) custom-call(f32[2,2,2,1,2048]{4,3,2,1,0:T(1,128)S(1)} %get-tuple-element.22.refs_0_, f32[2,4,32,1024]{3,2,1,0:T(8,128)S(1)} %copy-done.3), custom_call_target="tpu_custom_call" | custom-call | bytes 12000000 | tf_op jit(solution)/shard_map/edges/pallas_call | solution.py:88
  43.3 0.0 copy-done.2
  43.4 0.0 copy-done.5
  43.4 0.0 copy-start.7
  43.4 0.0 copy-start.10
  43.4 9.8 %forward.1 = (f32[2,128,2048]{2,1,0:T(8,128)S(1)}, f32[16,4,128]{2,1,0:T(4,128)S(1)}) custom-call(f32[2,2,128,2048]{3,2,1,0:T(8,128)S(1)} %get-tuple-element.21.field, f32[2,2,2,1,2048]{4,3,2,1,0:T(1,128)S(1)} %get-tuple-element.23.halo, bf16[1024,1024]{1,0:T(8,128)(2,1)S(1)} %get-tuple-element.24.even_hi, bf16[1024,1024]{1,0:T(8,128)(2,1)S(1)} %get-tuple-element.25.even_lo, ...), custom_call_target="tpu_custom_call" | custom-call | bytes 27000000 | tf_op jit(solution)/shard_map/forward/pallas_call | solution.py:661
  53.2 13.7 %join.1.incoming = f32[16,4,128]{2,1,0:T(4,128)S(1)} custom-call(f32[16,4,128]{2,1,0:T(4,128)S(1)} %get-tuple-element.29.ends, f32[16,17,128]{2,1,0:T(8,128)S(1)} %copy-done.7, f32[16,8,128]{2,1,0:T(8,128)S(1)} %copy-done.10), custom_call_target="tpu_custom_call" | custom-call | bytes 30000000 | tf_op jit(solution)/shard_map/join/pallas_call | solution.py:671
  67.0 6.8 %inverse.1 = f32[2,128,2048]{2,1,0:T(8,128)} custom-call(f32[2,128,2048]{2,1,0:T(8,128)S(1)} %get-tuple-element.28.value, f32[16,4,128]{2,1,0:T(4,128)S(1)} %join.1.incoming, bf16[1024,1024]{1,0:T(8,128)(2,1)S(1)} %get-tuple-element.24.even_hi, bf16[1024,1024]{1,0:T(8,128)(2,1)S(1)} %get-tuple-element.25.even_lo, ...), custom_call_target="tpu_custom_call" | custom-call | bytes 18000000 | tf_op jit(solution)/shard_map/inverse/pallas_call | solution.py:688
  (13 shorter events, 0.0 us)
Async XLA Ops:
  2.0 0.9 %copy-start.6 = (bf16[2,256,256]{2,1,0:T(8,128)(2,1)S(1)}, bf16[2,256,256]{2,1,0:T(8,128)(2,1)}, u32[]{:S(2)}) copy-start(bf16[2,256,256]{2,1,0:T(8,128)(2,1)} %param.14) | copy-start | bytes 786436
  7.3 0.6 copy-start.11
  7.9 10.7 %copy-start.4 = (f32[2,256,256]{2,1,0:T(8,128)S(1)}, f32[2,256,256]{2,1,0:T(8,128)}, u32[]{:S(2)}) copy-start(f32[2,256,256]{2,1,0:T(8,128)} %probe.1) | copy-start | bytes 1572868
  7.9 10.7 %copy-start.8 = (bf16[256,256]{1,0:T(8,128)(2,1)S(1)}, bf16[256,256]{1,0:T(8,128)(2,1)}, u32[]{:S(2)}) copy-start(bf16[256,256]{1,0:T(8,128)(2,1)} %constant.29.sin_ref) | copy-start | bytes 393220
  7.9 10.7 %copy-start.9 = (bf16[256,256]{1,0:T(8,128)(2,1)S(1)}, bf16[256,256]{1,0:T(8,128)(2,1)}, u32[]{:S(2)}) copy-start(bf16[256,256]{1,0:T(8,128)(2,1)} %constant.28.cos_ref) | copy-start | bytes 393220
  7.9 10.7 %copy-start.12 = (s32[3,3,3]{2,1,0:T(4,128)S(1)}, s32[3,3,3]{2,1,0:T(4,128)}, u32[]{:S(2)}) copy-start(s32[3,3,3]{2,1,0:T(4,128)} %copy-done.11) | copy-start | bytes 328
  12.1 1.1 %copy-start.1 = (bf16[3,2,2,128,256]{4,3,2,1,0:T(8,128)(2,1)S(1)}, bf16[3,2,2,128,256]{4,3,2,1,0:T(8,128)(2,1)}, u32[]{:S(2)}) copy-start(bf16[3,2,2,128,256]{4,3,2,1,0:T(8,128)(2,1)} %cut.1.refs_0_) | copy-start | bytes 2359300
  13.2 18.3 %copy-start = (f32[2,2,128,2048]{3,2,1,0:T(8,128)S(1)}, f32[2,2,128,2048]{3,2,1,0:T(8,128)}, u32[]{:S(2)}) copy-start(f32[2,2,128,2048]{3,2,1,0:T(8,128)} %field.3) | copy-start | bytes 12582916
  31.5 3.5 %copy-start.3 = (f32[2,4,32,1024]{3,2,1,0:T(8,128)S(1)}, f32[2,4,32,1024]{3,2,1,0:T(8,128)}, u32[]{:S(2)}) copy-start(f32[2,4,32,1024]{3,2,1,0:T(8,128)} %constant.16.clone.refs_1_) | copy-start | bytes 3145732
  31.6 11.8 %copy-start.2 = (f32[8,8,2048]{2,1,0:T(8,128)S(1)}, f32[8,8,2048]{2,1,0:T(8,128)}, u32[]{:S(2)}) copy-start(f32[8,8,2048]{2,1,0:T(8,128)} %constant.19.clone.local) | copy-start | bytes 1572868
  31.6 11.8 %copy-start.5 = (f32[8,2048]{1,0:T(8,128)S(1)}, f32[8,2048]{1,0:T(8,128)}, u32[]{:S(2)}) copy-start(f32[8,2048]{1,0:T(8,128)} %constant.20.clone.extra) | copy-start | bytes 196612
  43.4 9.9 %copy-start.7 = (f32[16,17,128]{2,1,0:T(8,128)S(1)}, f32[16,17,128]{2,1,0:T(8,128)}, u32[]{:S(2)}) copy-start(f32[16,17,128]{2,1,0:T(8,128)} %constant.21.clone.powers) | copy-start | bytes 417796
  43.4 9.9 %copy-start.10 = (f32[16,8,128]{2,1,0:T(8,128)S(1)}, f32[16,8,128]{2,1,0:T(8,128)}, u32[]{:S(2)}) copy-start(f32[16,8,128]{2,1,0:T(8,128)} %constant.22.clone.extra) | copy-start | bytes 196612
